TPU v7x, 128 devices: a whole 4x4x4 slice. The times are simulated.
128 devices in a mesh: row: 32 (over x, z, core), col: 4 (over y).
Axes of the slice: x: 4, y: 4, z: 4, core: 2. Of those that a mesh axis runs over, the one named last changes fastest.
Arguments:
- front: float32 [3, 32, 24, 4, 128, 128], P(None, 'row', None, 'col'), may hold values from -6 to 6
- child_tiles: float32 [8192, 128, 128], P(('row', 'col')), may hold values from -6 to 6
- tile_dest: int32 [8192, 1], P(('row', 'col')), may hold values from 0 to 127; in each aligned block of 64 rows (0 to 63, 64 to 127, ...) no two rows name the same one
- tile_slot: int32 [8192], P(('row', 'col')), may hold values from 0 to 71
- tile_count: int32 [128], P(('row', 'col')), may hold values from 48 to 64, as said below
- diag_inverses: float32 [2, 256, 256], replicated, as said below
Outputs:
- factored: float32 [3, 32, 24, 4, 128, 128], P(None, 'row', None, 'col')
Inputs may be any that keep to these rules, and one draw needn't show every extreme that they name: Among the 64 slots of one device, no two name the same device in tile_dest, live or not; every device is named by some slot. `tile_count`: some device has all 64 slots live. `diag_inverses`: each matrix is upper triangular with a positive diagonal; it is given as it is and need not match any diagonal block of the front.
All inputs are finite; a program needn't handle non-finite values.
Results may differ from a plain program's by a relative error of at most 0.000068.
Values sent between devices are 32-bit elements; how exact they have to be, the bound alone decides.
A program may use at most 128 MiB of HBM per device.

v0:
```python
import jax
import jax.numpy as jnp
from jax import lax
from jax.sharding import PartitionSpec as P


def panel_part(field, inverse, first, my_col, n_col):
    rows_here, tile = (field.shape[0], field.shape[2])
    total = jnp.zeros((rows_here * tile, 2 * tile), jnp.float32)
    for offset in range(2):
        target = first + offset
        local_b = target // n_col
        owner = target % n_col
        column = field[:, local_b].reshape(rows_here * tile, tile)
        term = jnp.dot(
            column, inverse[offset * tile : (offset + 1) * tile], precision=lax.Precision.HIGHEST
        )
        total = total + jnp.where(my_col == owner, term, jnp.zeros_like(term))
    return total


def panel_rows(field, inverse, first, my_row, my_col, n_row, n_col):
    rows_here, tile = (field.shape[0], field.shape[2])
    total = panel_part(field, inverse, first, my_col, n_col).reshape(rows_here, tile, 2 * tile)
    tile_row = jnp.arange(rows_here, dtype=jnp.int32) * n_row + my_row
    total = jnp.where((tile_row >= first)[:, None, None], total, jnp.zeros_like(total))
    summed = lax.psum(total, "col")
    return summed


def column_side(rows_three, cols_here, my_col, n_col):
    rows_here, tile = (rows_three.shape[0], rows_three.shape[1])
    whole = lax.all_gather(
        rows_three.reshape(rows_here, 1, tile, 2 * tile), "row", axis=1, tiled=True
    )
    ordered = whole.reshape(cols_here, n_col, tile, 2 * tile)
    return lax.dynamic_index_in_dim(ordered, my_col, axis=1, keepdims=False)


def trailing(field, rows_three, cols_three, limit, my_row, my_col, n_row, n_col):
    rows_here, cols_here = (field.shape[0], field.shape[1])
    tile_row = jnp.arange(rows_here, dtype=jnp.int32) * n_row + my_row
    tile_col = jnp.arange(cols_here, dtype=jnp.int32) * n_col + my_col
    keep = (tile_row >= limit)[:, None] & (tile_col >= limit)[None, :]
    update = jnp.einsum("aik,bjk->abij", rows_three, cols_three, precision=lax.Precision.HIGHEST)
    return field - jnp.where(keep[:, :, None, None], update, jnp.zeros_like(update))


def body(front, child_tiles, tile_dest, tile_slot, tile_count, diag_inverses):
    n_row = lax.axis_size("row")
    n_col = lax.axis_size("col")
    my_row = lax.axis_index("row")
    my_col = lax.axis_index("col")
    rows_here, cols_here, tile = (front.shape[0], front.shape[2], front.shape[4])
    slots = child_tiles.shape[0]
    devices = n_row * n_col
    live = jnp.arange(slots, dtype=jnp.int32) < tile_count[0]
    hits = (tile_dest[:, 0][None, :] == jnp.arange(devices, dtype=jnp.int32)[:, None]) & live[
        None, :
    ]
    found = jnp.any(hits, axis=1)
    picked = jnp.sum(hits.astype(jnp.int32) * jnp.arange(slots, dtype=jnp.int32)[None, :], axis=1)
    outgoing = jnp.take(child_tiles, picked, axis=0)
    outgoing = jnp.where(found[:, None, None], outgoing, jnp.zeros_like(outgoing))
    slot_out = jnp.where(found, jnp.take(tile_slot, picked).astype(jnp.float32), jnp.float32(-1.0))
    incoming, slot_in = (
        lax.all_to_all(outgoing, ("row", "col"), split_axis=0, concat_axis=0, tiled=True),
        lax.all_to_all(slot_out, ("row", "col"), split_axis=0, concat_axis=0, tiled=True),
    )
    placing = (
        slot_in[None, :] == jnp.arange(rows_here * cols_here, dtype=jnp.float32)[:, None]
    ).astype(jnp.float32)
    added = jnp.dot(
        placing, incoming.reshape(devices, tile * tile), precision=lax.Precision.HIGHEST
    )
    field = front[:, 0, :, 0] + added.reshape(rows_here, cols_here, tile, tile)
    rows_one = panel_rows(field, diag_inverses[0], 0, my_row, my_col, n_row, n_col)
    cols_one = column_side(rows_one, cols_here, my_col, n_col)
    field = trailing(field, rows_one, cols_one, 2, my_row, my_col, n_row, n_col)
    rows_two = panel_rows(field, diag_inverses[1], 2, my_row, my_col, n_row, n_col)
    cols_two = column_side(rows_two, cols_here, my_col, n_col)
    field = trailing(field, rows_two, cols_two, 4, my_row, my_col, n_row, n_col)
    for panel_index, rows_three in ((0, rows_one), (1, rows_two)):
        for offset in range(2):
            target = 2 * panel_index + offset
            local_b = target // n_col
            owner = target % n_col
            piece = rows_three[:, :, offset * tile : (offset + 1) * tile]
            field = field.at[:, local_b].set(jnp.where(my_col == owner, piece, field[:, local_b]))
    return field[:, None, :, None]


def solution(mesh):
    return jax.shard_map(
        body,
        mesh=mesh,
        in_specs=(
            P(None, "row", None, "col", None, None),
            P(("row", "col"), None, None),
            P(("row", "col"), None),
            P(("row", "col")),
            P(("row", "col")),
            P(),
        ),
        out_specs=P(None, "row", None, "col", None, None),
        check_vma=False,
    )
```

profile of v0, /device:TPU:1, one launch (start us, length us, event | category | flops | bytes accessed | tf_op | source)
XLA Modules:
  0.0 462.4 jit_solution(310653920112481245)
XLA Ops:
  6.5 0.0 copy-start
  7.2 0.8 select_reduce_fusion
  8.0 0.8 fusion.27
  8.8 0.0 copy-done
  8.8 1.2 gather_fusion
  10.0 0.7 copy.46
  10.8 11.5 %all-to-all-start = ((f32[128,1,1]{2,1,0:T(1,128)}), f32[128,1,1]{2,1,0:T(1,128)S(1)}, u32[]{:S(2)}, u32[]{:S(2)}) async-start(f32[128,1,1]{2,1,0:T(1,128)} %copy.46), calls=%async_computation | async-start | bytes 131072 | tf_op jit(solution)/shard_map/all_to_all | solution.py:68
  22.3 6.5 %gather_fusion.1 = f32[128,128,128]{2,1,0:T(8,128)} fusion(f32[64,128,128]{2,1,0:T(8,128)} %param.15, s32[1024]{0:T(1024)S(1)} %pad_clamp_fusion), kind=kCustom, calls=%fused_computation.1 | custom fusion | bytes 16777728 | tf_op jit(solution)/shard_map/jit(_take)/gather | solution.py:63
  28.8 6.4 %select_select_fusion = f32[128,128,128]{2,1,0:T(8,128)} fusion(f32[128,128,128]{2,1,0:T(8,128)} %gather_fusion.1, pred[128]{0:T(512)(128)(4,1)S(1)} %compare_and_fusion, pred[128]{0:T(512)(128)(4,1)S(1)} %fusion.27), kind=kLoop, calls=%fused_computation.4 | loop fusion | flops 4194304 | bytes 16777472 | tf_op jit(solution)/shard_map/jit(_where)/select_n | solution.py:64
  35.2 0.0 all-to-all-done
  35.2 10.2 %all-to-all-start.1 = ((f32[128,128,128]{2,1,0:T(8,128)}), f32[128,128,128]{2,1,0:T(8,128)}, u32[]{:S(2)}, u32[]{:S(2)}) async-start(f32[128,128,128]{2,1,0:T(8,128)} %select_select_fusion), calls=%async_computation.1 | async-start | bytes 16777216 | tf_op jit(solution)/shard_map/all_to_all | solution.py:67
  45.4 0.2 all-reduce.3.cloned.1.call-start
  45.7 1.0 reduce.8
  46.7 104.0 %all-to-all-done.1 = f32[128,128,128]{2,1,0:T(8,128)} async-done(((f32[128,128,128]{2,1,0:T(8,128)}), f32[128,128,128]{2,1,0:T(8,128)}, u32[]{:S(2)}, u32[]{:S(2)}) %all-to-all-start.1) | async-done | bytes 8388640 | tf_op jit(solution)/shard_map/all_to_all | solution.py:67
  150.8 9.3 %copy.58 = f32[128,128,128]{0,2,1:T(8,128)} copy(f32[128,128,128]{2,1,0:T(8,128)} %all-to-all-done.1) | data formatting | bytes 16777216 | tf_op jit(solution)/shard_map/reshape | solution.py:74
  160.1 0.0 copy-start.7
  160.1 12.3 %bitcast_add_fusion = f32[3,24,128,128]{3,1,2,0:T(8,128)S(1)} fusion(f32[3,1,24,1,128,128]{5,4,3,2,1,0:T(8,128)} %param.14, f32[128,128,128]{0,2,1:T(8,128)} %copy.58, f32[3,24]{1,0:T(4,128)S(1)} %multiply_add_fusion, f32[128]{0:T(128)S(1)} %reduce.8), kind=kOutput, calls=%fused_computation.9 | convolution fusion | flops 1813128192 | bytes 17826592 | tf_op jit(solution)/shard_map/dot_general | solution.py:73
  172.4 0.0 copy-start.3
  172.4 2.2 copy-done.3
  174.6 0.1 slice.175
  174.7 0.0 copy-done.7
  174.7 0.5 convolution_select_fusion.2
  175.2 0.5 fusion.12
  175.7 0.8 broadcast_select_fusion.1
  176.5 0.0 slice-start
  176.5 0.0 all-reduce.3.cloned.1.call-update
  176.5 0.0 all-gather.5.cloned.1.call-start
  176.6 37.1 %all-reduce.3.cloned.1.call-done = f32[3,128,256]{2,1,0:T(8,128)} async-done(((f32[3,128,256]{2,1,0:T(8,128)}), f32[3,128,256]{2,1,0:T(8,128)}) %all-reduce.3.cloned.1.call-update) | async-done | bytes 393232 | tf_op jit(solution)/shard_map/psum | solution.py:27
  213.7 0.0 all-gather.5.cloned.1.call-update
  213.7 0.3 all-reduce.5.cloned.1.call-start
  214.0 0.1 broadcast_and_fusion.1
  214.1 68.0 %all-gather.5.cloned.1.call-done = f32[3,4096,256]{2,1,0:T(8,128)} async-done(((f32[3,128,256]{2,1,0:T(8,128)}), f32[3,4096,256]{2,1,0:T(8,128)}) %all-gather.5.cloned.1.call-update) | async-done | bytes 12582928 | tf_op jit(solution)/shard_map/all_gather | solution.py:33
  282.1 0.0 slice-start.1
  282.1 6.4 %fusion.6 = f32[24,128,3,128]{1,3,2,0:T(8,128)S(1)} fusion(f32[24,4,128,256]{3,2,1,0:T(8,128)} %bitcast.106, s32[]{:T(128)S(6)} %select_n.140, f32[3,128,256]{2,1,0:T(8,128)} %all-reduce.3.cloned.1.call-done), kind=kOutput, calls=%fused_computation.12 | convolution fusion | flops 3623878656 | bytes 8257540 | tf_op jit(solution)/shard_map/aik,bjk->abij/dot_general | solution.py:45
  288.5 0.0 slice-done
  288.6 0.0 slice-done.1
  288.6 3.2 fusion.3
  291.8 0.0 copy-start.4
  291.8 2.2 copy-done.4
  294.0 0.1 slice.176
  294.1 0.5 convolution_select_fusion
  294.5 0.5 fusion.13
  295.0 0.8 broadcast_select_fusion
  295.9 0.0 all-reduce.5.cloned.1.call-update
  295.9 0.3 all-gather.7.cloned.1.call-start
  296.2 39.0 %all-reduce.5.cloned.1.call-done = f32[3,128,256]{2,1,0:T(8,128)} async-done(((f32[3,128,256]{2,1,0:T(8,128)}), f32[3,128,256]{2,1,0:T(8,128)}) %all-reduce.5.cloned.1.call-update) | async-done | bytes 393232 | tf_op jit(solution)/shard_map/psum | solution.py:27
  335.2 0.0 all-gather.7.cloned.1.call-update
  335.3 0.1 broadcast_and_fusion
  335.3 68.1 %all-gather.7.cloned.1.call-done = f32[3,4096,256]{2,1,0:T(8,128)} async-done(((f32[3,128,256]{2,1,0:T(8,128)}), f32[3,4096,256]{2,1,0:T(8,128)}) %all-gather.7.cloned.1.call-update) | async-done | bytes 12582928 | tf_op jit(solution)/shard_map/all_gather | solution.py:33
  403.5 8.3 %fusion.4 = f32[24,128,3,128]{3,1,2,0:T(8,128)} fusion(f32[24,4,128,256]{3,2,1,0:T(8,128)} %bitcast.107, s32[]{:T(128)S(6)} %select_n.140, f32[3,128,256]{2,1,0:T(8,128)} %all-reduce.5.cloned.1.call-done), kind=kOutput, calls=%fused_computation.10 | convolution fusion | flops 3623878656 | bytes 8257540 | tf_op jit(solution)/shard_map/aik,bjk->abij/dot_general | solution.py:45
  411.8 6.1 %copy.49 = f32[24,128,3,128]{1,0,3,2:T(8,128)} copy(f32[24,128,3,128]{3,1,2,0:T(8,128)} %fusion.4) | data formatting | bytes 9437184 | tf_op jit(solution)/shard_map/aik,bjk->abij/dot_general | solution.py:45
  417.8 4.4 fusion.2
  422.2 0.0 copy-start.2
  422.2 2.1 copy-done.2
  424.3 0.1 slice.178
  424.4 0.0 copy-done.5
  424.4 0.0 copy-done.6
  424.4 0.1 slice_select_fusion
  424.5 6.5 %scatter.14 = f32[3,1,24,1,128,128]{5,2,4,0,3,1:T(8,128)} dynamic-update-slice(f32[3,1,24,1,128,128]{5,2,4,0,3,1:T(8,128)} %bitcast.97, f32[3,1,1,1,128,128]{5,2,4,0,3,1:T(1,128)S(1)} %bitcast.111, s32[]{:T(128)} %constant.145.clone.1, s32[]{:T(128)} %constant.145.clone.1, s32[]{:T(128)} %constant.145.clone.1, s32[]{:T(128)} %constant.145.clone.1, s32[]{:T(128)} %constant.145.clone.1, ...) | dynamic-update-slice | bytes 393220 | tf_op jit(solution)/shard_map/scatter | solution.py:89
  431.0 6.5 %scatter.15 = f32[3,1,24,1,128,128]{5,2,4,0,3,1:T(8,128)} dynamic-update-slice(f32[3,1,24,1,128,128]{5,2,4,0,3,1:T(8,128)} %scatter.14, f32[3,1,1,1,128,128]{5,2,4,0,3,1:T(1,128)S(1)} %bitcast.110, s32[]{:T(128)} %constant.145.clone.1, s32[]{:T(128)} %constant.145.clone.1, s32[]{:T(128)} %constant.145.clone.1, s32[]{:T(128)} %constant.145.clone.1, s32[]{:T(128)} %constant.145.clone.1, ...) | dynamic-update-slice | bytes 393220 | tf_op jit(solution)/shard_map/scatter | solution.py:89
  437.5 6.5 %scatter.16 = f32[3,1,24,1,128,128]{5,2,4,0,3,1:T(8,128)} dynamic-update-slice(f32[3,1,24,1,128,128]{5,2,4,0,3,1:T(8,128)} %scatter.15, f32[3,1,1,1,128,128]{5,2,4,0,3,1:T(1,128)S(1)} %bitcast.109, s32[]{:T(128)} %constant.145.clone.1, s32[]{:T(128)} %constant.145.clone.1, s32[]{:T(128)} %constant.145.clone.1, s32[]{:T(128)} %constant.145.clone.1, s32[]{:T(128)} %constant.145.clone.1, ...) | dynamic-update-slice | bytes 393220 | tf_op jit(solution)/shard_map/scatter | solution.py:89
  444.0 6.5 %scatter.19 = f32[3,1,24,1,128,128]{5,2,4,0,3,1:T(8,128)} dynamic-update-slice(f32[3,1,24,1,128,128]{5,2,4,0,3,1:T(8,128)} %scatter.16, f32[3,1,1,1,128,128]{5,2,4,0,3,1:T(1,128)S(1)} %bitcast.108, s32[]{:T(128)} %constant.145.clone.1, s32[]{:T(128)} %constant.145.clone.1, s32[]{:T(128)} %constant.145.clone.1, s32[]{:T(128)} %constant.145.clone.1, s32[]{:T(128)} %constant.145.clone.1, ...) | dynamic-update-slice | bytes 393220 | tf_op jit(solution)/shard_map/scatter | solution.py:89
  450.5 5.3 %copy.54 = f32[3,1,24,1,128,128]{5,4,3,2,1,0:T(8,128)} copy(f32[3,1,24,1,128,128]{5,2,4,0,3,1:T(8,128)} %scatter.19) | data formatting | bytes 9437184 | tf_op jit(solution)/shard_map/scatter | solution.py:89
  455.8 0.0 copy-done.1
  (15 shorter events, 0.1 us)
Async XLA Ops:
  6.5 2.2 copy-start
  10.8 24.5 %all-to-all-start = ((f32[128,1,1]{2,1,0:T(1,128)}), f32[128,1,1]{2,1,0:T(1,128)S(1)}, u32[]{:S(2)}, u32[]{:S(2)}) async-start(f32[128,1,1]{2,1,0:T(1,128)} %copy.46), calls=%async_computation | async-start | bytes 131072 | tf_op jit(solution)/shard_map/all_to_all | solution.py:68
  35.2 115.6 %all-to-all-start.1 = ((f32[128,128,128]{2,1,0:T(8,128)}), f32[128,128,128]{2,1,0:T(8,128)}, u32[]{:S(2)}, u32[]{:S(2)}) async-start(f32[128,128,128]{2,1,0:T(8,128)} %select_select_fusion), calls=%async_computation.1 | async-start | bytes 16777216 | tf_op jit(solution)/shard_map/all_to_all | solution.py:67
  45.4 168.2 %all-reduce.3.cloned.1.call-start = ((), (), s32[]{:S(2)}) async-start(), calls=%async_computation.2 | async-start | bytes 786432 | tf_op jit(solution)/shard_map/psum | solution.py:27
  160.1 14.6 %copy-start.7 = (f32[2,256,256]{2,1,0:T(8,128)S(1)}, f32[2,256,256]{2,1,0:T(8,128)}, u32[]{:S(2)}) copy-start(f32[2,256,256]{2,1,0:T(8,128)} %param.19) | copy-start | bytes 1572868
  172.4 2.2 copy-start.3
  176.5 112.0 %slice-start = ((s8[4718592]{0:T(1024)(128)(4,1)}), s8[524288]{0:T(1024)(128)(4,1)S(1)}, s32[]{:S(2)}) async-start(s8[4718592]{0:T(1024)(128)(4,1)} %bitcast.98), calls=%async_computation.6 | async-start | bytes 1048576
  176.5 105.5 %all-gather.5.cloned.1.call-start = ((), (), s32[]{:S(2)}) async-start(), calls=%async_computation.4 | async-start | bytes 12976128 | tf_op jit(solution)/shard_map/all_gather | solution.py:33
  213.7 121.5 %all-reduce.5.cloned.1.call-start = ((), (), s32[]{:S(2)}) async-start(), calls=%async_computation.3 | async-start | bytes 786432 | tf_op jit(solution)/shard_map/psum | solution.py:27
  282.1 6.5 %slice-start.1 = ((s8[4718592]{0:T(1024)(128)(4,1)}), s8[4194304]{0:T(1024)(128)(4,1)S(1)}, s32[]{:S(2)}) async-start(s8[4718592]{0:T(1024)(128)(4,1)} %bitcast.98), calls=%async_computation.7 | async-start | bytes 8388608
  291.8 2.2 copy-start.4
  295.9 107.6 %all-gather.7.cloned.1.call-start = ((), (), s32[]{:S(2)}) async-start(), calls=%async_computation.5 | async-start | bytes 12976128 | tf_op jit(solution)/shard_map/all_gather | solution.py:33
  417.8 6.6 %copy-start.5 = (f32[3,128,256]{2,1,0:T(8,128)S(1)}, f32[3,128,256]{2,1,0:T(8,128)}, u32[]{:S(2)}) copy-start(f32[3,128,256]{2,1,0:T(8,128)} %all-reduce.3.cloned.1.call-done) | copy-start | bytes 1179652
  417.8 6.6 %copy-start.6 = (f32[3,128,256]{2,1,0:T(8,128)S(1)}, f32[3,128,256]{2,1,0:T(8,128)}, u32[]{:S(2)}) copy-start(f32[3,128,256]{2,1,0:T(8,128)} %all-reduce.5.cloned.1.call-done) | copy-start | bytes 1179652
  422.2 2.1 copy-start.2
  444.0 11.8 %copy-start.1 = (s32[64]{0:T(128)S(1)}, s32[64]{0:T(128)}, u32[]{:S(2)}) copy-start(s32[64]{0:T(128)} %param.17) | copy-start | bytes 772
Sparse Core Ops, SparseCore 0:
  176.7 36.9 all-reduce.2
  216.0 66.0 all-gather.4
  296.0 39.1 all-reduce.4
  337.4 66.0 all-gather.6
where the time goes:
time: 463 us; the launch traced here: 462 us
  waiting for transfers between devices  316 us (68%)
  local copies, waits for them, and re-layouts  61.9 us (13%)
  matrix products  28.9 us (6%)
  starting transfers between devices  22.5 us (5%)
  other arithmetic  18.5 us (4%)
  between operations  14.1 us (3%)
    all_gather x2, waiting for transfers between devices, column_side(): lax.all_gather(rows_three.reshape(rows_here, 1, tile, 2 * tile), 'row', a...  136 us
    all_to_all x1, waiting for transfers between devices, body(): lax.all_to_all(outgoing, ('row', 'col'), split_axis=0, concat_axis=0, til...  104 us
    psum x2, waiting for transfers between devices, panel_rows(): summed = lax.psum(total, 'col')  76.1 us
    scatter x5, local copies, waits for them, and re-layouts, body(): field.at[:, local_b]  31.3 us
    dot_general x2, matrix products, trailing(): jnp.einsum('aik,bjk->abij', rows_three, cols_three, precision=lax.Precisi...  14.7 us
    dot_general x1, matrix products, body(): jnp.dot(placing, incoming.reshape(devices, tile * tile), precision=lax.Pr...  12.3 us
    all_to_all x1, starting transfers between devices, body(): lax.all_to_all(slot_out, ('row', 'col'), split_axis=0, concat_axis=0, til...  11.5 us
    all_to_all x1, starting transfers between devices, body(): lax.all_to_all(outgoing, ('row', 'col'), split_axis=0, concat_axis=0, til...  10.2 us
  transfers between devices with their start and end apart: 6, of which 5 were waited for; matrix products, arithmetic and copies ran while one was open for 3% of the time, Pallas kernels for 0%

commit v1 on v0

v1 whole, which is shorter than its diff:
```python
import itertools

import jax
import jax.numpy as jnp
from jax import lax
from jax.experimental import pallas as pl
from jax.experimental.pallas import tpu as pltpu
from jax.sharding import PartitionSpec as P

MESH = pl.DeviceIdType.MESH
F32 = jnp.float32
BF16 = jnp.bfloat16
VMEM_LIMIT = 60 * 2**20
TILE = 128
SHARD = 200


def place(r, c):
    return r // 8, c, (r // 2) % 4, r % 2


def device(x, y, z, k):
    return x * 8 + z * 2 + k, y


def shift(r, c, o):
    x, y, z, k = place(r, c)
    return device((x + o[0]) % 4, (y + o[1]) % 4, (z + o[2]) % 4, (k + o[3]) % 2)


def exchange_order():
    def negated(o):
        return (-o[0]) % 4, (-o[1]) % 4, (-o[2]) % 4, o[3]

    orbits, seen = [], set()
    for o in itertools.product(range(4), range(4), range(4), range(2)):
        if o in seen or o == (0, 0, 0, 0):
            continue
        orbit, a = [], o
        for _ in range(3):
            for b in (a, negated(a)):
                if b not in orbit:
                    orbit.append(b)
            a = (a[1], a[2], a[0], a[3])
        seen |= set(orbit)
        orbits.append(orbit)
    far = sorted(orbits, key=lambda orbit: -sum(min(v, 4 - v) for v in orbit[0][:3]))
    order = []
    while far:
        order += far.pop(0)
        if far:
            order += far.pop(-1)
    return order


ORDER = exchange_order()


def signal(sem, dev):
    pl.semaphore_signal(sem, inc=1, device_id=dev, device_id_type=MESH)


def enter(r, c, line_sem, column_sem):
    barrier = pltpu.get_barrier_semaphore()
    plane = [shift(r, c, (0, 0, dz, dk)) for dz in range(4) for dk in range(2) if dz or dk]
    lines = [shift(r, c, (d, 0, 0, 0)) for d in (1, 2, 3)]
    columns = [shift(r, c, (0, d, 0, 0)) for d in (1, 2, 3)]
    for dev in plane + lines + columns:
        signal(barrier, dev)
    pl.semaphore_wait(barrier, 13)
    for dev in lines:
        signal(line_sem, dev)
    pl.semaphore_wait(line_sem, 3)
    for dev in columns:
        signal(column_sem, dev)
    pl.semaphore_wait(column_sem, 3)


def remote(src, dst, send, recv, dev):
    return pltpu.make_async_remote_copy(
        src_ref=src, dst_ref=dst, send_sem=send, recv_sem=recv, device_id=dev, device_id_type=MESH
    )


def wait_bytes(ref, sem):
    pltpu.make_async_copy(ref, ref, sem).wait()


def exchange_kernel(
    code_ref, code_rows, child_ref, in_ref, codes_ref, packed, line_sem, column_sem, send_sem, recv_sem, code_send, code_recv, own_sem
):
    r = lax.axis_index("row")
    c = lax.axis_index("col")
    me = r * 4 + c
    enter(r, c, line_sem, column_sem)

    for o in ORDER:
        pr, pc = shift(r, c, o)
        remote(
            code_rows.at[pr * 4 + pc], codes_ref.at[me], code_send, code_recv, (pr, pc)
        ).start()
    own_code = pltpu.make_async_copy(code_rows.at[me], codes_ref.at[me], own_sem)
    own_code.start()

    def pack(i, dev_index):
        slot = jnp.maximum(code_ref[dev_index] - 1, 0) % 64
        packed[i] = child_ref[slot]

    for i, o in enumerate(ORDER):
        pr, pc = shift(r, c, o)
        pack(i, pr * 4 + pc)
        remote(packed.at[i], in_ref.at[me], send_sem, recv_sem, (pr, pc)).start()
    last = len(ORDER)
    pack(last, me)
    own_tile = pltpu.make_async_copy(packed.at[last], in_ref.at[me], own_sem)
    own_code.wait()
    own_tile.start()
    own_tile.wait()

    wait_bytes(code_rows.at[pl.ds(0, last)], code_send)
    wait_bytes(codes_ref.at[pl.ds(0, last)], code_recv)
    wait_bytes(packed.at[pl.ds(0, last)], send_sem)
    wait_bytes(in_ref.at[pl.ds(0, last)], recv_sem)


def exchange(code, code_rows, child):
    any_space = pl.BlockSpec(memory_space=pl.ANY)
    vmem = pl.BlockSpec(memory_space=pltpu.VMEM)
    return pl.pallas_call(
        exchange_kernel,
        out_shape=(
            jax.ShapeDtypeStruct((128, TILE, TILE), F32),
            jax.ShapeDtypeStruct((128, 1, 128), jnp.int32),
        ),
        in_specs=[pl.BlockSpec(memory_space=pltpu.SMEM), vmem, vmem],
        out_specs=(any_space, vmem),
        scratch_shapes=[
            pltpu.VMEM((128, TILE, TILE), F32),
            pltpu.SemaphoreType.REGULAR,
            pltpu.SemaphoreType.REGULAR,
        ]
        + [pltpu.SemaphoreType.DMA] * 5,
        compiler_params=pltpu.CompilerParams(
            collective_id=0, has_side_effects=True, vmem_limit_bytes=VMEM_LIMIT
        ),
        name="exchange",
    )(code, code_rows, child)


STEP = 8


def add_kernel(codes_ref, front_ref, in_ref, out_ref, sem, front_sem):
    i = pl.program_id(0)

    @pl.when(i == 0)
    def _():
        copy = pltpu.make_async_copy(front_ref, out_ref, front_sem)
        copy.start()
        copy.wait()

    for s in range(STEP):
        code = codes_ref[i * STEP + s]

        @pl.when(code > 0)
        def _():
            q = (code - 1) // 64
            out_ref[q] += in_ref[s]


def add_tiles(codes, front, incoming):
    return pl.pallas_call(
        add_kernel,
        grid=(128 // STEP,),
        out_shape=jax.ShapeDtypeStruct(front.shape, F32),
        in_specs=[
            pl.BlockSpec(memory_space=pltpu.SMEM),
            pl.BlockSpec(memory_space=pl.ANY),
            pl.BlockSpec((STEP, TILE, TILE), lambda i: (i, 0, 0)),
        ],
        out_specs=pl.BlockSpec(front.shape, lambda i: (0, 0, 0)),
        scratch_shapes=[pltpu.SemaphoreType.DMA, pltpu.SemaphoreType.DMA],
        compiler_params=pltpu.CompilerParams(vmem_limit_bytes=VMEM_LIMIT),
        name="add_tiles",
    )(codes, front, incoming)


def halves(a):
    high = a.astype(BF16)
    return high, (a - high.astype(F32)).astype(BF16)


def dot3(a, b, dims=((1,), (0,))):
    ah, al = a if isinstance(a, tuple) else halves(a)
    bh, bl = b if isinstance(b, tuple) else halves(b)

    def dot(u, v):
        return lax.dot_general(u, v, (dims, ((), ())), preferred_element_type=F32)

    return dot(ah, bh) + (dot(ah, bl) + dot(al, bh))


def panel_kernel(
    field_ref,
    diag_ref,
    all_ref,
    own_ref,
    tiles,
    quarter,
    corner,
    shard,
    line_sem,
    column_sem,
    load_sem,
    local_sem,
    q_send,
    q_recv,
    c_send,
    c_recv,
    o_send,
    o_recv,
    first_recv,
    second_recv,
    twin_recv,
    g_send,
):
    r = lax.axis_index("row")
    c = lax.axis_index("col")
    x, _, z, k = place(r, c)
    load = pltpu.make_async_copy(field_ref.at[:, 0], tiles, load_sem)
    load.start()
    enter(r, c, line_sem, column_sem)
    load.wait()

    target_col = r % 4
    for j in range(4):
        target_row = (r // 4) * 4 + j
        mine = (target_row == r) & (target_col == c)
        src = tiles.at[:, pl.ds(32 * j, 32), :]

        @pl.when(mine)
        def _():
            pltpu.make_async_copy(src, quarter.at[c], q_recv).start()

        @pl.when(jnp.logical_not(mine))
        def _():
            remote(src, quarter.at[c], q_send, q_recv, (target_row, target_col)).start()

    sends_corner = ((r == 2) | (r == 3)) & (c < 2)

    @pl.when(sends_corner)
    def _():
        @pl.loop(0, 64)
        def _(n):
            i = n // 4
            tr = i + 16 * (r - 2)
            tc = n % 4
            src = tiles.at[0, pl.ds(pl.multiple_of(i * 8, 8), 8), :]
            mine = (tr == r) & (tc == c)

            @pl.when(mine)
            def _():
                pltpu.make_async_copy(src, corner.at[c], c_recv).start()

            @pl.when(jnp.logical_not(mine))
            def _():
                remote(src, corner.at[c], c_send, c_recv, (tr, tc)).start()

    wait_bytes(quarter, q_recv)
    wait_bytes(corner, c_recv)

    for d in (1, 3, 2):
        remote(tiles, own_ref.at[c], o_send, o_recv, (r, (c + d) % 4)).start()
    own = pltpu.make_async_copy(tiles, own_ref.at[c], local_sem.at[0])
    own.start()

    left = jnp.concatenate([quarter[0].reshape(96, TILE), quarter[1].reshape(96, TILE)], axis=1)
    extra = jnp.concatenate([corner[0], corner[1]], axis=1)
    shard[0:104, :] = dot3(jnp.concatenate([left, extra], axis=0), diag_ref[0])
    right = jnp.concatenate([quarter[2].reshape(96, TILE), quarter[3].reshape(96, TILE)], axis=1)
    shard[104:200, :] = dot3(right, diag_ref[1])

    def first(d):
        return (((x + (1 - k) * d) % 4) * 8 + ((z + k * d) % 4) * 2 + k, c)

    def second(e):
        return (((x + k * e) % 4) * 8 + ((z + (1 - k) * e) % 4) * 2 + k, c)

    twin = (r + 1 - 2 * k, c)
    for d in (1, 3, 2):
        remote(shard, all_ref.at[r], g_send, first_recv.at[d - 1], first(d)).start()
    for e in (1, 3, 2):
        remote(shard, all_ref.at[r], g_send, second_recv.at[e - 1], second(e)).start()
    remote(shard, all_ref.at[r], g_send, twin_recv, twin).start()
    keep = pltpu.make_async_copy(shard, all_ref.at[r], local_sem.at[1])
    keep.start()
    for d in (1, 3, 2):
        source = first(4 - d)[0]
        block = all_ref.at[source]
        wait_bytes(block, first_recv.at[d - 1])
        for e in (1, 3, 2):
            remote(block, block, g_send, second_recv.at[d * 3 + e - 1], second(e)).start()
        remote(block, block, g_send, twin_recv, twin).start()
    for d in (0, 1, 3, 2):
        for e in (1, 3, 2):
            sx = (x - (1 - k) * d - k * e + 8) % 4
            sz = (z - k * d - (1 - k) * e + 8) % 4
            block = all_ref.at[sx * 8 + sz * 2 + k]
            wait_bytes(block, second_recv.at[d * 3 + e - 1])
            remote(block, block, g_send, twin_recv, twin).start()
    wait_bytes(all_ref.at[pl.ds(0, 16)], twin_recv)
    wait_bytes(all_ref.at[pl.ds(0, 31)], g_send)
    keep.wait()
    own.wait()
    wait_bytes(own_ref.at[pl.ds(0, 3)], o_send)
    wait_bytes(own_ref.at[pl.ds(0, 3)], o_recv)

    row_quarter = tiles.at[:, pl.ds(0, 32), :]
    holds_one = (r % 4) == c
    for j in range(4):

        @pl.when(jnp.logical_not(holds_one & ((r % 4) == j)))
        def _():
            wait_bytes(row_quarter, q_send)

    @pl.when(sends_corner)
    def _():
        @pl.loop(0, 63)
        def _(n):
            wait_bytes(corner.at[0], c_send)

        @pl.when(r == 3)
        def _():
            wait_bytes(corner.at[0], c_send)


def gather_panels(field, diag):
    any_space = pl.BlockSpec(memory_space=pl.ANY)
    vmem = pl.BlockSpec(memory_space=pltpu.VMEM)
    dma = pltpu.SemaphoreType.DMA
    return pl.pallas_call(
        panel_kernel,
        out_shape=(
            jax.ShapeDtypeStruct((32, SHARD, 256), F32),
            jax.ShapeDtypeStruct((4, 3, TILE, TILE), F32),
        ),
        in_specs=[any_space, vmem],
        out_specs=(any_space, any_space),
        scratch_shapes=[
            pltpu.VMEM((3, TILE, TILE), F32),
            pltpu.VMEM((4, 3, 32, TILE), F32),
            pltpu.VMEM((2, 8, TILE), F32),
            pltpu.VMEM((SHARD, 256), F32),
            pltpu.SemaphoreType.REGULAR,
            pltpu.SemaphoreType.REGULAR,
            dma,
            dma((2,)),
            dma,
            dma,
            dma,
            dma,
            dma,
            dma,
            dma((3,)),
            dma((12,)),
            dma,
            dma,
        ],
        compiler_params=pltpu.CompilerParams(
            collective_id=1, has_side_effects=True, vmem_limit_bytes=VMEM_LIMIT
        ),
        name="gather_panels",
    )(field, diag)


def update_kernel(field_ref, all_ref, corner_ref, own_ref, diag_ref, out_ref, row_high, row_low, mix):
    g = pl.program_id(0)
    a = pl.program_id(1)
    r = lax.axis_index("row")
    c = lax.axis_index("col")

    @pl.when((g == 0) & (a == 0))
    def _():
        corner = corner_ref[...].reshape(256, 256)
        one, two = halves(diag_ref[0]), halves(diag_ref[1])
        both = dot3(corner, two, ((0,), (0,)))
        mix[0], mix[1] = halves(both)
        left = jnp.concatenate([own_ref[0].reshape(384, TILE), own_ref[1].reshape(384, TILE)], axis=1)
        right = jnp.concatenate([own_ref[2].reshape(384, TILE), own_ref[3].reshape(384, TILE)], axis=1)
        p_one = dot3(left, one)
        p_two = dot3(right, two) - dot3(p_one, halves(both))
        tile_row = (lax.broadcasted_iota(jnp.int32, (384, 1), 0) // TILE) * 32 + r
        zero = jnp.zeros_like(p_one)
        p_two = jnp.where(tile_row >= 2, p_two, zero)
        panel = jnp.where(
            c < 2,
            jnp.where(c == 0, p_one[:, :TILE], p_one[:, TILE:]),
            jnp.where(c == 2, p_two[:, :TILE], p_two[:, TILE:]),
        )
        out_ref[...] = panel.reshape(3, 1, TILE, TILE)
        rows = jnp.concatenate(
            [jnp.where(tile_row >= 2, p_one, zero), jnp.where(tile_row >= 4, p_two, zero)], axis=1
        )
        row_high[...], row_low[...] = halves(rows)

    @pl.when((g > 0) | (a > 0))
    def _():
        start = pl.multiple_of(a * 32, 32)
        later = pl.multiple_of(a * 32 + 104, 8)
        k_one = all_ref[0, :, pl.ds(start, 32), :].reshape(TILE, 256)
        base = all_ref[0, :, pl.ds(later, 32), :].reshape(TILE, 256)
        k_two = base - dot3(k_one, (mix[0], mix[1]))
        cols = halves(jnp.concatenate([k_one, k_two], axis=1))
        product = dot3((row_high[...], row_low[...]), cols, ((1,), (1,)))
        out_ref[...] = field_ref[...] - product.reshape(3, 1, TILE, TILE)


def update(field, gathered, own, diag):
    whole = lambda shape: pl.BlockSpec(shape, lambda g, a: (0,) * len(shape))
    tiles = pl.BlockSpec((3, 1, TILE, TILE), lambda g, a: (0, a * 8 + g, 0, 0))
    corner = gathered[:, 96:104, :]
    return pl.pallas_call(
        update_kernel,
        grid=(8, 3),
        out_shape=jax.ShapeDtypeStruct(field.shape, F32),
        in_specs=[
            tiles,
            pl.BlockSpec((1, 4, SHARD, 256), lambda g, a: (g, 0, 0, 0)),
            whole((32, 8, 256)),
            whole((4, 3, TILE, TILE)),
            whole((2, 256, 256)),
        ],
        out_specs=tiles,
        scratch_shapes=[
            pltpu.VMEM((384, 512), BF16),
            pltpu.VMEM((384, 512), BF16),
            pltpu.VMEM((2, 256, 256), BF16),
        ],
        compiler_params=pltpu.CompilerParams(vmem_limit_bytes=VMEM_LIMIT),
        name="update",
    )(field, gathered.reshape(8, 4, SHARD, 256), corner, own, diag)


def body(front, child_tiles, tile_dest, tile_slot, tile_count, diag_inverses):
    slot = jnp.arange(64, dtype=jnp.int32)
    hits = (tile_dest[:, 0][None, :] == jnp.arange(128, dtype=jnp.int32)[:, None]) & (slot < tile_count[0])[None, :]
    code = jnp.sum(jnp.where(hits, (tile_slot * 64 + slot + 1)[None, :], 0), axis=1)
    code_rows = jnp.broadcast_to(code[:, None, None], (128, 1, 128))
    incoming, codes = exchange(code, code_rows, child_tiles)
    field = add_tiles(codes[:, 0, 0], front.reshape(72, TILE, TILE), incoming).reshape(3, 24, TILE, TILE)
    gathered, own = gather_panels(field, diag_inverses)
    return update(field, gathered, own, diag_inverses).reshape(front.shape)


def solution(mesh):
    return jax.shard_map(
        body,
        mesh=mesh,
        in_specs=(
            P(None, "row", None, "col", None, None),
            P(("row", "col"), None, None),
            P(("row", "col"), None),
            P(("row", "col")),
            P(("row", "col")),
            P(),
        ),
        out_specs=P(None, "row", None, "col", None, None),
        check_vma=False,
    )
```

time: 463 us -> 211 us (0.46)
  waiting for transfers between devices: 316 us -> 0 us
  Pallas kernels: 0 us -> 202 us
  local copies, waits for them, and re-layouts: 61.9 us -> 6.31 us
  matrix products: 28.9 us -> 0 us
  starting transfers between devices: 22.5 us -> 0 us
  other arithmetic: 18.5 us -> 1.43 us
  between operations: 14.1 us -> 0.69 us
    pallas_call x0 -> x4, Pallas kernels: none -> 202 us  [the longest x1 113 us: exchange(): pl.pallas_call(exchange_kernel, out_shape=(jax.ShapeDtypeStruct((128, TIL...]
    all_gather x2 -> x0, waiting for transfers between devices: 136 us -> none  [column_side(): lax.all_gather(rows_three.reshape(rows_here, 1, tile, 2 * tile), 'row', a...]
    all_to_all x2 -> x0, waiting for transfers between devices: 104 us -> none  [the longest x1 104 us: body(): lax.all_to_all(outgoing, ('row', 'col'), split_axis=0, concat_axis=0, til...]
    psum x2 -> x0, waiting for transfers between devices: 76.1 us -> none  [panel_rows(): summed = lax.psum(total, 'col')]
    scatter x5 -> x0, local copies, waits for them, and re-layouts: 31.3 us -> none  [body(): field.at[:, local_b]]
    dot_general x7 -> x0, matrix products: 28.9 us -> none  [the longest x2 14.7 us: trailing(): jnp.einsum('aik,bjk->abij', rows_three, cols_three, precision=lax.Precisi...]
    all_to_all x2 -> x0, starting transfers between devices: 21.7 us -> none  [the longest x1 11.5 us: body(): lax.all_to_all(slot_out, ('row', 'col'), split_axis=0, concat_axis=0, til...]
    reshape x1 -> x0, local copies, waits for them, and re-layouts: 9.29 us -> none  [body(): incoming.reshape(devices, tile * tile)]
  transfers between devices with their start and end apart: 6 -> 0, of which waited for: 5 -> 0; matrix products, arithmetic and copies ran while one was open for 3% -> 0% of each run, Pallas kernels for 0% -> 0%
where the time goes in v1:
time: 211 us; the launch traced here: 210 us
  Pallas kernels  202 us (96%)
  local copies, waits for them, and re-layouts  6.31 us (3%)
    pallas_call x1, Pallas kernels, exchange(): pl.pallas_call(exchange_kernel, out_shape=(jax.ShapeDtypeStruct((128, TIL...  113 us
    pallas_call x1, Pallas kernels, gather_panels(): pl.pallas_call(panel_kernel, out_shape=(jax.ShapeDtypeStruct((32, SHARD,...  49.4 us
    pallas_call x1, Pallas kernels, update(): pl.pallas_call(update_kernel, grid=(8, 3), out_shape=jax.ShapeDtypeStruct...  24.6 us
    pallas_call x1, Pallas kernels, add_tiles(): pl.pallas_call(add_kernel, grid=(128 // STEP,), out_shape=jax.ShapeDtypeS...  14.3 us

profile of v1, /device:TPU:1, one launch (start us, length us, event | category | flops | bytes accessed | tf_op | source)
XLA Modules:
  0.0 210.0 jit_solution(6741491955410738610)
XLA Ops:
  0.7 0.7 add_add_fusion
  1.3 0.8 select_reduce_fusion.code_ref
  2.1 0.0 copy-start
  2.1 0.8 broadcast_in_dim.23.code_rows
  2.9 0.0 copy-done
  2.9 113.4 %exchange.1 = (f32[128,128,128]{2,1,0:T(8,128)}, s32[128,1,128]{2,1,0:T(1,128)}) custom-call(s32[128]{0:T(128)} %copy-done, s32[128,1,128]{2,1,0:T(1,128)} %broadcast_in_dim.23.code_rows, f32[64,128,128]{2,1,0:T(8,128)} %child_ref.1), custom_call_target="tpu_custom_call" | custom-call | tf_op jit(solution)/shard_map/exchange/pallas_call | solution.py:129
  116.4 3.8 %slice_reduce_fusion.codes_ref = s32[128]{0:T(128)} fusion(s32[128,1,128]{2,1,0:T(1,128)} %get-tuple-element.9), kind=kLoop, calls=%fused_computation | loop fusion | bytes 1024 | tf_op jit(solution)/shard_map/slice | solution.py:450
  120.2 14.3 %add_tiles.1 = f32[72,128,128]{2,1,0:T(8,128)} custom-call(s32[128]{0:T(128)} %slice_reduce_fusion.codes_ref, f32[72,128,128]{2,1,0:T(8,128)} %bitcast.12, f32[128,128,128]{2,1,0:T(8,128)} %get-tuple-element.10.in_ref), custom_call_target="tpu_custom_call" | custom-call | tf_op jit(solution)/shard_map/add_tiles/pallas_call | solution.py:172
  134.4 49.4 %gather_panels.1 = (f32[32,200,256]{2,1,0:T(8,128)}, f32[4,3,128,128]{3,2,1,0:T(8,128)}) custom-call(f32[3,24,128,128]{3,2,1,0:T(8,128)} %bitcast.9, f32[2,256,256]{2,1,0:T(8,128)} %diag_ref.3), custom_call_target="tpu_custom_call" | custom-call | tf_op jit(solution)/shard_map/gather_panels/pallas_call | solution.py:341
  183.8 1.7 slice.7.corner_ref
  185.5 24.6 %update.1 = f32[3,24,128,128]{3,2,1,0:T(8,128)} custom-call(f32[3,24,128,128]{3,2,1,0:T(8,128)} %bitcast.10, f32[8,4,200,256]{3,2,1,0:T(8,128)} %bitcast.11, f32[32,8,256]{2,1,0:T(8,128)} %slice.7.corner_ref, f32[4,3,128,128]{3,2,1,0:T(8,128)} %get-tuple-element.12.own_ref, f32[2,256,256]{2,1,0:T(8,128)} %diag_ref.3), custom_call_target="tpu_custom_call" | custom-call | tf_op jit(solution)/shard_map/update/pallas_call | solution.py:422
  (1 shorter events, 0.0 us)
Async XLA Ops:
  2.1 0.8 copy-start

commit v2 on v1

--- a/solution.py
+++ b/solution.py
@@ -86,105 +86,6 @@
     pltpu.make_async_copy(ref, ref, sem).wait()
 
 
-def exchange_kernel(
-    code_ref, code_rows, child_ref, in_ref, codes_ref, packed, line_sem, column_sem, send_sem, recv_sem, code_send, code_recv, own_sem
-):
-    r = lax.axis_index("row")
-    c = lax.axis_index("col")
-    me = r * 4 + c
-    enter(r, c, line_sem, column_sem)
-
-    for o in ORDER:
-        pr, pc = shift(r, c, o)
-        remote(
-            code_rows.at[pr * 4 + pc], codes_ref.at[me], code_send, code_recv, (pr, pc)
-        ).start()
-    own_code = pltpu.make_async_copy(code_rows.at[me], codes_ref.at[me], own_sem)
-    own_code.start()
-
-    def pack(i, dev_index):
-        slot = jnp.maximum(code_ref[dev_index] - 1, 0) % 64
-        packed[i] = child_ref[slot]
-
-    for i, o in enumerate(ORDER):
-        pr, pc = shift(r, c, o)
-        pack(i, pr * 4 + pc)
-        remote(packed.at[i], in_ref.at[me], send_sem, recv_sem, (pr, pc)).start()
-    last = len(ORDER)
-    pack(last, me)
-    own_tile = pltpu.make_async_copy(packed.at[last], in_ref.at[me], own_sem)
-    own_code.wait()
-    own_tile.start()
-    own_tile.wait()
-
-    wait_bytes(code_rows.at[pl.ds(0, last)], code_send)
-    wait_bytes(codes_ref.at[pl.ds(0, last)], code_recv)
-    wait_bytes(packed.at[pl.ds(0, last)], send_sem)
-    wait_bytes(in_ref.at[pl.ds(0, last)], recv_sem)
-
-
-def exchange(code, code_rows, child):
-    any_space = pl.BlockSpec(memory_space=pl.ANY)
-    vmem = pl.BlockSpec(memory_space=pltpu.VMEM)
-    return pl.pallas_call(
-        exchange_kernel,
-        out_shape=(
-            jax.ShapeDtypeStruct((128, TILE, TILE), F32),
-            jax.ShapeDtypeStruct((128, 1, 128), jnp.int32),
-        ),
-        in_specs=[pl.BlockSpec(memory_space=pltpu.SMEM), vmem, vmem],
-        out_specs=(any_space, vmem),
-        scratch_shapes=[
-            pltpu.VMEM((128, TILE, TILE), F32),
-            pltpu.SemaphoreType.REGULAR,
-            pltpu.SemaphoreType.REGULAR,
-        ]
-        + [pltpu.SemaphoreType.DMA] * 5,
-        compiler_params=pltpu.CompilerParams(
-            collective_id=0, has_side_effects=True, vmem_limit_bytes=VMEM_LIMIT
-        ),
-        name="exchange",
-    )(code, code_rows, child)
-
-
-STEP = 8
-
-
-def add_kernel(codes_ref, front_ref, in_ref, out_ref, sem, front_sem):
-    i = pl.program_id(0)
-
-    @pl.when(i == 0)
-    def _():
-        copy = pltpu.make_async_copy(front_ref, out_ref, front_sem)
-        copy.start()
-        copy.wait()
-
-    for s in range(STEP):
-        code = codes_ref[i * STEP + s]
-
-        @pl.when(code > 0)
-        def _():
-            q = (code - 1) // 64
-            out_ref[q] += in_ref[s]
-
-
-def add_tiles(codes, front, incoming):
-    return pl.pallas_call(
-        add_kernel,
-        grid=(128 // STEP,),
-        out_shape=jax.ShapeDtypeStruct(front.shape, F32),
-        in_specs=[
-            pl.BlockSpec(memory_space=pltpu.SMEM),
-            pl.BlockSpec(memory_space=pl.ANY),
-            pl.BlockSpec((STEP, TILE, TILE), lambda i: (i, 0, 0)),
-        ],
-        out_specs=pl.BlockSpec(front.shape, lambda i: (0, 0, 0)),
-        scratch_shapes=[pltpu.SemaphoreType.DMA, pltpu.SemaphoreType.DMA],
-        compiler_params=pltpu.CompilerParams(vmem_limit_bytes=VMEM_LIMIT),
-        name="add_tiles",
-    )(codes, front, incoming)
-
-
 def halves(a):
     high = a.astype(BF16)
     return high, (a - high.astype(F32)).astype(BF16)
@@ -200,18 +101,48 @@
     return dot(ah, bh) + (dot(ah, bl) + dot(al, bh))
 
 
-def panel_kernel(
-    field_ref,
+def to_rows(column):
+    down = lax.broadcasted_iota(jnp.int32, (128, 128), 0)
+    across = lax.broadcasted_iota(jnp.int32, (128, 128), 1)
+    return jnp.sum(jnp.where(down == across, column, 0), axis=0, keepdims=True)
+
+
+def assemble_kernel(
+    count_ref,
+    dest_ref,
+    slot_ref,
+    child_hbm,
+    front_hbm,
     diag_ref,
+    field_out,
     all_ref,
     own_ref,
+    child,
+    field,
+    packed,
+    incoming,
+    code_rows,
+    code_in,
+    rows,
+    sorted_rows,
+    picks,
+    order,
     tiles,
     quarter,
     corner,
     shard,
     line_sem,
     column_sem,
-    load_sem,
+    child_sem,
+    front_sem,
+    rows_sem,
+    order_sem,
+    tile_send,
+    tile_recv,
+    code_send,
+    code_recv,
+    keep_sem,
+    out_sem,
     local_sem,
     q_send,
     q_recv,
@@ -227,10 +158,79 @@
     r = lax.axis_index("row")
     c = lax.axis_index("col")
     x, _, z, k = place(r, c)
-    load = pltpu.make_async_copy(field_ref.at[:, 0], tiles, load_sem)
-    load.start()
+    me = r * 4 + c
+    child_load = pltpu.make_async_copy(child_hbm, child, child_sem)
+    child_load.start()
+    front_load = pltpu.make_async_copy(front_hbm, field, front_sem)
+    front_load.start()
+
+    down = lax.broadcasted_iota(jnp.int32, (128, 64), 0)
+    slot = lax.broadcasted_iota(jnp.int32, (128, 64), 1)
+    hits = (dest_ref[...] == down) & (slot < count_ref[0])
+    code = jnp.sum(jnp.where(hits, slot_ref[...] * 64 + slot + 1, 0), axis=1, keepdims=True)
+    code = jnp.broadcast_to(code, (128, 128))
+    code_rows[...] = code.reshape(128, 1, 128)
+    rows[0:1, :] = jnp.maximum(to_rows(code) - 1, 0) % 64
+    to_scalars = pltpu.make_async_copy(rows, picks, rows_sem)
+    to_scalars.start()
     enter(r, c, line_sem, column_sem)
-    load.wait()
+    to_scalars.wait()
+    child_load.wait()
+
+    for o in ORDER:
+        pr, pc = shift(r, c, o)
+        remote(
+            code_rows.at[pr * 4 + pc], code_in.at[me], code_send, code_recv, (pr, pc)
+        ).start()
+    code_in[pl.ds(me, 1)] = code_rows[pl.ds(me, 1)]
+    for i, o in enumerate(ORDER):
+        pr, pc = shift(r, c, o)
+        packed[i] = child[picks[0, pr * 4 + pc]]
+        remote(packed.at[i], incoming.at[me], tile_send, tile_recv, (pr, pc)).start()
+    last = len(ORDER)
+    incoming[pl.ds(me, 1)] = child[picks[0, me]].reshape(1, TILE, TILE)
+
+    wait_bytes(code_in.at[pl.ds(0, last)], code_recv)
+    wait_bytes(code_rows.at[pl.ds(0, last)], code_send)
+    got = code_in[...].reshape(128, 128)
+    down = lax.broadcasted_iota(jnp.int32, (128, 128), 0)
+    across = lax.broadcasted_iota(jnp.int32, (128, 128), 1)
+    place_in = jnp.where(got > 0, (got - 1) // 64, 127)
+    key = place_in * 128 + down
+    smaller = to_rows(key) < key
+    rank = jnp.sum(smaller.astype(jnp.int32), axis=1, keepdims=True)
+    at_rank = rank == across
+    source = jnp.sum(jnp.where(at_rank, down, 0), axis=0, keepdims=True)
+    in_order = jnp.sum(jnp.where(at_rank, place_in, 0), axis=0, keepdims=True)
+    before = jnp.sum(jnp.where(rank + 1 == across, place_in, 0), axis=0, keepdims=True)
+    starts = (in_order != before) | (lax.broadcasted_iota(jnp.int32, (1, 128), 1) == 0)
+    up_to = jnp.sum((place_in <= across).astype(jnp.int32), axis=0, keepdims=True)
+    equal = jnp.sum((place_in == across).astype(jnp.int32), axis=0, keepdims=True)
+    sorted_rows[0:1, :] = source
+    sorted_rows[1:2, :] = starts.astype(jnp.int32)
+    sorted_rows[2:3, :] = jnp.maximum(up_to - 1, 0)
+    sorted_rows[3:4, :] = equal
+    to_scalars = pltpu.make_async_copy(sorted_rows, order, order_sem)
+    to_scalars.start()
+    to_scalars.wait()
+    front_load.wait()
+    wait_bytes(packed.at[pl.ds(0, last)], tile_send)
+    wait_bytes(incoming.at[pl.ds(0, last)], tile_recv)
+
+    def run(t, total):
+        tile = incoming[order[0, t]]
+        total = jnp.where(order[1, t] > 0, tile, total + tile)
+        packed[t] = total
+        return total
+
+    lax.fori_loop(0, 128, run, jnp.zeros((TILE, TILE), F32))
+
+    def assembled(q):
+        added = packed[order[2, q]]
+        return field[q] + jnp.where(order[3, q] > 0, added, 0.0)
+
+    for a in range(3):
+        tiles[a] = assembled(a * 24)
 
     target_col = r % 4
     for j in range(4):
@@ -266,6 +266,14 @@
             def _():
                 remote(src, corner.at[c], c_send, c_recv, (tr, tc)).start()
 
+    for a in range(3):
+
+        @pl.loop(1, 24)
+        def _(b):
+            field[a * 24 + b] = assembled(a * 24 + b)
+
+    field_store = pltpu.make_async_copy(field, field_out, out_sem)
+    field_store.start()
     wait_bytes(quarter, q_recv)
     wait_bytes(corner, c_recv)
 
@@ -311,6 +319,7 @@
     wait_bytes(all_ref.at[pl.ds(0, 16)], twin_recv)
     wait_bytes(all_ref.at[pl.ds(0, 31)], g_send)
     keep.wait()
+    field_store.wait()
     own.wait()
     wait_bytes(own_ref.at[pl.ds(0, 3)], o_send)
     wait_bytes(own_ref.at[pl.ds(0, 3)], o_recv)
@@ -334,52 +343,55 @@
             wait_bytes(corner.at[0], c_send)
 
 
-def gather_panels(field, diag):
+def assemble(count, dest, slot, child, front, diag):
     any_space = pl.BlockSpec(memory_space=pl.ANY)
     vmem = pl.BlockSpec(memory_space=pltpu.VMEM)
+    smem = pl.BlockSpec(memory_space=pltpu.SMEM)
     dma = pltpu.SemaphoreType.DMA
     return pl.pallas_call(
-        panel_kernel,
+        assemble_kernel,
         out_shape=(
+            jax.ShapeDtypeStruct((72, TILE, TILE), F32),
             jax.ShapeDtypeStruct((32, SHARD, 256), F32),
             jax.ShapeDtypeStruct((4, 3, TILE, TILE), F32),
         ),
-        in_specs=[any_space, vmem],
-        out_specs=(any_space, any_space),
+        in_specs=[smem, vmem, vmem, any_space, any_space, vmem],
+        out_specs=(any_space,) * 3,
         scratch_shapes=[
+            pltpu.VMEM((64, TILE, TILE), F32),
+            pltpu.VMEM((72, TILE, TILE), F32),
+            pltpu.VMEM((128, TILE, TILE), F32),
+            pltpu.VMEM((128, TILE, TILE), F32),
+            pltpu.VMEM((128, 1, 128), jnp.int32),
+            pltpu.VMEM((128, 1, 128), jnp.int32),
+            pltpu.VMEM((8, 128), jnp.int32),
+            pltpu.VMEM((8, 128), jnp.int32),
+            pltpu.SMEM((8, 128), jnp.int32),
+            pltpu.SMEM((8, 128), jnp.int32),
             pltpu.VMEM((3, TILE, TILE), F32),
             pltpu.VMEM((4, 3, 32, TILE), F32),
             pltpu.VMEM((2, 8, TILE), F32),
             pltpu.VMEM((SHARD, 256), F32),
             pltpu.SemaphoreType.REGULAR,
             pltpu.SemaphoreType.REGULAR,
-            dma,
-            dma((2,)),
-            dma,
-            dma,
-            dma,
-            dma,
-            dma,
-            dma,
-            dma((3,)),
-            dma((12,)),
-            dma,
-            dma,
-        ],
+        ]
+        + [dma] * 10
+        + [dma((2,))]
+        + [dma] * 6
+        + [dma((3,)), dma((12,)), dma, dma],
         compiler_params=pltpu.CompilerParams(
-            collective_id=1, has_side_effects=True, vmem_limit_bytes=VMEM_LIMIT
+            collective_id=0, has_side_effects=True, vmem_limit_bytes=VMEM_LIMIT
         ),
-        name="gather_panels",
-    )(field, diag)
+        name="assemble",
+    )(count, dest, slot, child, front, diag)
 
 
 def update_kernel(field_ref, all_ref, corner_ref, own_ref, diag_ref, out_ref, row_high, row_low, mix):
     g = pl.program_id(0)
-    a = pl.program_id(1)
     r = lax.axis_index("row")
     c = lax.axis_index("col")
 
-    @pl.when((g == 0) & (a == 0))
+    @pl.when(g == 0)
     def _():
         corner = corner_ref[...].reshape(256, 256)
         one, two = halves(diag_ref[0]), halves(diag_ref[1])
@@ -397,35 +409,48 @@
             jnp.where(c == 0, p_one[:, :TILE], p_one[:, TILE:]),
             jnp.where(c == 2, p_two[:, :TILE], p_two[:, TILE:]),
         )
-        out_ref[...] = panel.reshape(3, 1, TILE, TILE)
+        out_ref[:, 0, 0] = panel.reshape(3, TILE, TILE)
         rows = jnp.concatenate(
             [jnp.where(tile_row >= 2, p_one, zero), jnp.where(tile_row >= 4, p_two, zero)], axis=1
         )
         row_high[...], row_low[...] = halves(rows)
 
-    @pl.when((g > 0) | (a > 0))
-    def _():
-        start = pl.multiple_of(a * 32, 32)
-        later = pl.multiple_of(a * 32 + 104, 8)
-        k_one = all_ref[0, :, pl.ds(start, 32), :].reshape(TILE, 256)
-        base = all_ref[0, :, pl.ds(later, 32), :].reshape(TILE, 256)
+    def columns(first):
+        n = 3 - first
+        k_one = jnp.concatenate(
+            [all_ref[0, :, 32 * b : 32 * b + 32, :].reshape(TILE, 256) for b in range(first, 3)]
+        )
+        base = jnp.concatenate(
+            [all_ref[0, :, 32 * b + 104 : 32 * b + 136, :].reshape(TILE, 256) for b in range(first, 3)]
+        )
         k_two = base - dot3(k_one, (mix[0], mix[1]))
         cols = halves(jnp.concatenate([k_one, k_two], axis=1))
         product = dot3((row_high[...], row_low[...]), cols, ((1,), (1,)))
-        out_ref[...] = field_ref[...] - product.reshape(3, 1, TILE, TILE)
+        for b in range(n):
+            part = product[:, TILE * b : TILE * b + TILE].reshape(3, TILE, TILE)
+            out_ref[:, first + b, 0] = field_ref[:, first + b, 0] - part
+
+    @pl.when(g == 0)
+    def _():
+        columns(1)
+
+    @pl.when(g > 0)
+    def _():
+        columns(0)
 
 
 def update(field, gathered, own, diag):
-    whole = lambda shape: pl.BlockSpec(shape, lambda g, a: (0,) * len(shape))
-    tiles = pl.BlockSpec((3, 1, TILE, TILE), lambda g, a: (0, a * 8 + g, 0, 0))
+    whole = lambda shape: pl.BlockSpec(shape, lambda g: (0,) * len(shape))
+    tiles = pl.BlockSpec((3, 3, 1, TILE, TILE), lambda g: (0, 0, g, 0, 0))
     corner = gathered[:, 96:104, :]
+    shape = (3, 3, 8, TILE, TILE)
     return pl.pallas_call(
         update_kernel,
-        grid=(8, 3),
-        out_shape=jax.ShapeDtypeStruct(field.shape, F32),
+        grid=(8,),
+        out_shape=jax.ShapeDtypeStruct(shape, F32),
         in_specs=[
             tiles,
-            pl.BlockSpec((1, 4, SHARD, 256), lambda g, a: (g, 0, 0, 0)),
+            pl.BlockSpec((1, 4, SHARD, 256), lambda g: (g, 0, 0, 0)),
             whole((32, 8, 256)),
             whole((4, 3, TILE, TILE)),
             whole((2, 256, 256)),
@@ -438,17 +463,18 @@
         ],
         compiler_params=pltpu.CompilerParams(vmem_limit_bytes=VMEM_LIMIT),
         name="update",
-    )(field, gathered.reshape(8, 4, SHARD, 256), corner, own, diag)
+    )(field.reshape(shape), gathered.reshape(8, 4, SHARD, 256), corner, own, diag)
 
 
 def body(front, child_tiles, tile_dest, tile_slot, tile_count, diag_inverses):
-    slot = jnp.arange(64, dtype=jnp.int32)
-    hits = (tile_dest[:, 0][None, :] == jnp.arange(128, dtype=jnp.int32)[:, None]) & (slot < tile_count[0])[None, :]
-    code = jnp.sum(jnp.where(hits, (tile_slot * 64 + slot + 1)[None, :], 0), axis=1)
-    code_rows = jnp.broadcast_to(code[:, None, None], (128, 1, 128))
-    incoming, codes = exchange(code, code_rows, child_tiles)
-    field = add_tiles(codes[:, 0, 0], front.reshape(72, TILE, TILE), incoming).reshape(3, 24, TILE, TILE)
-    gathered, own = gather_panels(field, diag_inverses)
+    field, gathered, own = assemble(
+        tile_count,
+        tile_dest.reshape(1, 64),
+        tile_slot.reshape(1, 64),
+        child_tiles,
+        front.reshape(72, TILE, TILE),
+        diag_inverses,
+    )
     return update(field, gathered, own, diag_inverses).reshape(front.shape)
 
 

time: 211 us -> 168 us (0.80)
  Pallas kernels: 202 us -> 163 us
  local copies, waits for them, and re-layouts: 6.31 us -> 1.67 us
    pallas_call x4 -> x2, Pallas kernels: 202 us -> 163 us  [the longest x1 149 us: assemble(): pl.pallas_call(assemble_kernel, out_shape=(jax.ShapeDtypeStruct((72, TILE...]
    slice x1 -> x0, local copies, waits for them, and re-layouts: 3.8 us -> none  [body(): codes[:, 0, 0]]
where the time goes in v2:
time: 168 us; the launch traced here: 165 us
  Pallas kernels  163 us (97%)
    pallas_call x1, Pallas kernels, assemble(): pl.pallas_call(assemble_kernel, out_shape=(jax.ShapeDtypeStruct((72, TILE...  149 us
    pallas_call x1, Pallas kernels, update(): pl.pallas_call(update_kernel, grid=(8,), out_shape=jax.ShapeDtypeStruct(s...  14.5 us

profile of v2, /device:TPU:1, one launch (start us, length us, event | category | flops | bytes accessed | tf_op | source)
XLA Modules:
  0.0 165.4 jit_solution(13303945828605328846)
XLA Ops:
  0.7 148.5 %assemble.1 = (f32[72,128,128]{2,1,0:T(8,128)}, f32[32,200,256]{2,1,0:T(8,128)}, f32[4,3,128,128]{3,2,1,0:T(8,128)}) custom-call(s32[1]{0:T(128)S(6)} %copy.8.count_ref, s32[1,64]{1,0:T(1,128)} %bitcast.11, s32[1,64]{1,0:T(1,128)} %bitcast.12, f32[64,128,128]{2,1,0:T(8,128)} %child_hbm.1, f32[72,128,128]{2,1,0:T(8,128)} %bitcast.9, f32[2,256,256]{2,1,0:T(8,128)} %diag_ref.3), custom_call_target="tpu_custom_call" | custom-call | tf_op jit(solution)/shard_map/assemble/pallas_call | solution.py:351
  149.2 1.7 %slice.3.corner_ref = f32[32,8,256]{2,1,0:T(8,128)} slice(f32[32,200,256]{2,1,0:T(8,128)} %get-tuple-element.9), slice={[0:32], [96:104], [0:256]} | slice | bytes 524288 | tf_op jit(solution)/shard_map/slice | solution.py:445
  150.8 14.5 %update.1 = f32[3,3,8,128,128]{4,3,2,1,0:T(8,128)} custom-call(f32[3,3,8,128,128]{4,3,2,1,0:T(8,128)} %bitcast.10, f32[8,4,200,256]{3,2,1,0:T(8,128)} %bitcast.8, f32[32,8,256]{2,1,0:T(8,128)} %slice.3.corner_ref, f32[4,3,128,128]{3,2,1,0:T(8,128)} %get-tuple-element.10.own_ref, f32[2,256,256]{2,1,0:T(8,128)} %diag_ref.3), custom_call_target="tpu_custom_call" | custom-call | tf_op jit(solution)/shard_map/update/pallas_call | solution.py:447

commit v3 on v2

v3 whole, which is shorter than its diff:
```python
import itertools

import jax
import jax.numpy as jnp
from jax import lax
from jax.experimental import pallas as pl
from jax.experimental.pallas import tpu as pltpu
from jax.sharding import PartitionSpec as P

MESH = pl.DeviceIdType.MESH
F32 = jnp.float32
BF16 = jnp.bfloat16
VMEM_LIMIT = 40 * 2**20
TILE = 128
FIRST = 12
EARLY = 96
HALF = ((0, 104), (104, 96))
SHARD = 200


def place(r, c):
    return r // 8, c, (r // 2) % 4, r % 2


def device(x, y, z, k):
    return x * 8 + z * 2 + k, y


def shift(r, c, o):
    x, y, z, k = place(r, c)
    return device((x + o[0]) % 4, (y + o[1]) % 4, (z + o[2]) % 4, (k + o[3]) % 2)


def exchange_order():
    def negated(o):
        return (-o[0]) % 4, (-o[1]) % 4, (-o[2]) % 4, o[3]

    orbits, seen = [], set()
    for o in itertools.product(range(4), range(4), range(4), range(2)):
        if o in seen or o == (0, 0, 0, 0):
            continue
        orbit, a = [], o
        for _ in range(3):
            for b in (a, negated(a)):
                if b not in orbit:
                    orbit.append(b)
            a = (a[1], a[2], a[0], a[3])
        seen |= set(orbit)
        orbits.append(orbit)
    far = sorted(orbits, key=lambda orbit: -sum(min(v, 4 - v) for v in orbit[0][:3]))
    order = []
    while far:
        order += far.pop(0)
        if far:
            order += far.pop(-1)
    return order


ORDER = exchange_order()


def signal(sem, dev):
    pl.semaphore_signal(sem, inc=1, device_id=dev, device_id_type=MESH)


def enter(r, c, line_sem, column_sem):
    barrier = pltpu.get_barrier_semaphore()
    plane = [shift(r, c, (0, 0, dz, dk)) for dz in range(4) for dk in range(2) if dz or dk]
    lines = [shift(r, c, (d, 0, 0, 0)) for d in (1, 2, 3)]
    columns = [shift(r, c, (0, d, 0, 0)) for d in (1, 2, 3)]
    for dev in plane + lines + columns:
        signal(barrier, dev)
    pl.semaphore_wait(barrier, 13)
    for dev in lines:
        signal(line_sem, dev)
    pl.semaphore_wait(line_sem, 3)
    for dev in columns:
        signal(column_sem, dev)
    pl.semaphore_wait(column_sem, 3)


def remote(src, dst, send, recv, dev):
    return pltpu.make_async_remote_copy(
        src_ref=src, dst_ref=dst, send_sem=send, recv_sem=recv, device_id=dev, device_id_type=MESH
    )


def wait_bytes(ref, sem):
    pltpu.make_async_copy(ref, ref, sem).wait()


def halves(a):
    high = a.astype(BF16)
    return high, (a - high.astype(F32)).astype(BF16)


def dot3(a, b, dims=((1,), (0,))):
    ah, al = a if isinstance(a, tuple) else halves(a)
    bh, bl = b if isinstance(b, tuple) else halves(b)

    def dot(u, v):
        return lax.dot_general(u, v, (dims, ((), ())), preferred_element_type=F32)

    if dims == ((1,), (0,)):
        return dot(jnp.concatenate([ah, ah, al], axis=1), jnp.concatenate([bh, bl, bh], axis=0))
    return dot(ah, bh) + (dot(ah, bl) + dot(al, bh))


def to_rows(column):
    down = lax.broadcasted_iota(jnp.int32, (128, 128), 0)
    across = lax.broadcasted_iota(jnp.int32, (128, 128), 1)
    return jnp.sum(jnp.where(down == across, column, 0), axis=0, keepdims=True)


def assemble_kernel(
    count_ref,
    dest_hbm,
    slot_hbm,
    child_hbm,
    front_hbm,
    diag_hbm,
    field,
    all_ref,
    rows_ref,
    diag_ref,
    dest_ref,
    slot_ref,
    child,
    packed,
    incoming,
    incoming_late,
    own_ref,
    code_rows,
    code_in,
    rows,
    sorted_rows,
    picks,
    order,
    tiles,
    quarter,
    corner,
    line_sem,
    column_sem,
    small_sem,
    child_sem,
    front_sem,
    diag_sem,
    rows_sem,
    order_sem,
    tile_send,
    tile_recv,
    late_recv,
    code_send,
    code_recv,
    own_sem,
    q_send,
    q_recv,
    c_send,
    c_recv,
    o_send,
    o_recv,
    first_recv,
    second_recv,
    twin_recv,
    g_send,
):
    r = lax.axis_index("row")
    c = lax.axis_index("col")
    x, _, z, k = place(r, c)
    me = r * 4 + c
    loads = [
        pltpu.make_async_copy(dest_hbm, dest_ref, small_sem.at[0]),
        pltpu.make_async_copy(slot_hbm, slot_ref, small_sem.at[1]),
    ]
    for load in loads:
        load.start()
    child_load = pltpu.make_async_copy(child_hbm, child, child_sem)
    child_load.start()
    front_load = pltpu.make_async_copy(front_hbm, field, front_sem)
    front_load.start()
    diag_load = pltpu.make_async_copy(diag_hbm, diag_ref, diag_sem)
    diag_load.start()
    for load in loads:
        load.wait()

    down = lax.broadcasted_iota(jnp.int32, (128, 64), 0)
    slot = lax.broadcasted_iota(jnp.int32, (128, 64), 1)
    hits = (dest_ref[...] == down) & (slot < count_ref[0])
    code = jnp.sum(jnp.where(hits, slot_ref[...] * 64 + slot + 1, 0), axis=1, keepdims=True)
    code = jnp.broadcast_to(code, (128, 128))
    code_rows[...] = code.reshape(128, 1, 128)
    rows[0:1, :] = jnp.maximum(to_rows(code) - 1, 0) % 64
    to_scalars = pltpu.make_async_copy(rows, picks, rows_sem)
    to_scalars.start()
    enter(r, c, line_sem, column_sem)
    to_scalars.wait()
    child_load.wait()

    def send_codes():
        for i, o in enumerate(ORDER):
            pr, pc = shift(r, c, o)
            remote(code_rows.at[pr * 4 + pc], code_in.at[i], code_send, code_recv, (pr, pc)).start()

    for i, o in enumerate(ORDER):
        if i == FIRST:
            send_codes()
        pr, pc = shift(r, c, o)
        packed[i] = child[picks[0, pr * 4 + pc]]
        landing, recv = (incoming.at[i], tile_recv) if i < EARLY else (incoming_late.at[i - EARLY], late_recv)
        remote(packed.at[i], landing, tile_send, recv, (pr, pc)).start()
    last = len(ORDER)
    code_in[last] = code_rows[me]
    incoming_late[last - EARLY] = child[picks[0, me]]

    wait_bytes(code_in.at[pl.ds(0, last)], code_recv)
    wait_bytes(code_rows.at[pl.ds(0, last)], code_send)
    got = code_in[...].reshape(128, 128)
    down = lax.broadcasted_iota(jnp.int32, (128, 128), 0)
    across = lax.broadcasted_iota(jnp.int32, (128, 128), 1)
    late = (down >= EARLY).astype(jnp.int32)
    place_in = jnp.where(got > 0, (got - 1) // 64, 127)
    group = late * 128 + place_in
    key = group * 128 + down
    smaller = to_rows(key) < key
    rank = jnp.sum(smaller.astype(jnp.int32), axis=1, keepdims=True)
    source = jnp.sum(jnp.where(rank == across, down, 0), axis=0, keepdims=True)
    in_order = jnp.sum(jnp.where(rank == across, group, 0), axis=0, keepdims=True)
    before = jnp.sum(jnp.where(rank + 1 == across, group, 0), axis=0, keepdims=True)
    first = lax.broadcasted_iota(jnp.int32, (1, 128), 1) == 0
    sorted_rows[0:1, :] = source % EARLY
    sorted_rows[1:2, :] = ((in_order != before) | first).astype(jnp.int32)
    for n in range(2):
        up_to = jnp.sum((group <= across + 128 * n).astype(jnp.int32), axis=0, keepdims=True)
        equal = jnp.sum((group == across + 128 * n).astype(jnp.int32), axis=0, keepdims=True)
        sorted_rows[2 + n : 3 + n, :] = jnp.maximum(up_to - 1 - EARLY * n, 0)
        sorted_rows[4 + n : 5 + n, :] = equal
    to_scalars = pltpu.make_async_copy(sorted_rows, order, order_sem)
    to_scalars.start()
    to_scalars.wait()
    front_load.wait()
    diag_load.wait()
    wait_bytes(packed.at[pl.ds(0, last)], tile_send)

    def sums(buffer, start, count):
        def run(t, total):
            tile = buffer[order[0, t]]
            total = jnp.where(order[1, t] > 0, tile, total + tile)
            packed[t] = total
            return total

        lax.fori_loop(start, start + count, run, jnp.zeros((TILE, TILE), F32))

    def assembled(q, n):
        added = packed.at[pl.ds(EARLY * n, (EARLY, 128 - EARLY)[n])][order[2 + n, q]]
        return field[q] + jnp.where(order[4 + n, q] > 0, added, 0.0)

    wait_bytes(incoming, tile_recv)
    sums(incoming, 0, EARLY)

    @pl.loop(0, 72)
    def _(q):
        field[q] = assembled(q, 0)

    wait_bytes(incoming_late.at[pl.ds(0, last - EARLY)], late_recv)
    sums(incoming_late, EARLY, 128 - EARLY)
    for a in range(3):
        tiles[a] = assembled(a * 24, 1)

    target_col = r % 4
    for j in range(4):
        target_row = (r // 4) * 4 + j
        mine = (target_row == r) & (target_col == c)
        src = tiles.at[:, pl.ds(32 * j, 32), :]

        @pl.when(mine)
        def _():
            pltpu.make_async_copy(src, quarter.at[c], q_recv).start()

        @pl.when(jnp.logical_not(mine))
        def _():
            remote(src, quarter.at[c], q_send, q_recv, (target_row, target_col)).start()

    sends_corner = ((r == 2) | (r == 3)) & (c < 2)

    @pl.when(sends_corner)
    def _():
        @pl.loop(0, 64)
        def _(n):
            i = n // 4
            tr = i + 16 * (r - 2)
            tc = n % 4
            src = tiles.at[0, pl.ds(pl.multiple_of(i * 8, 8), 8), :]
            mine = (tr == r) & (tc == c)

            @pl.when(mine)
            def _():
                pltpu.make_async_copy(src, corner.at[c], c_recv).start()

            @pl.when(jnp.logical_not(mine))
            def _():
                remote(src, corner.at[c], c_send, c_recv, (tr, tc)).start()

    for a in range(3):

        @pl.loop(1, 24)
        def _(b):
            field[a * 24 + b] = assembled(a * 24 + b, 1)

    wait_bytes(quarter, q_recv)
    wait_bytes(corner, c_recv)

    for d in (1, 3, 2):
        remote(tiles, own_ref.at[c], o_send, o_recv, (r, (c + d) % 4)).start()
    own = pltpu.make_async_copy(tiles, own_ref.at[c], own_sem)
    own.start()

    left = jnp.concatenate([quarter[0].reshape(96, TILE), quarter[1].reshape(96, TILE)], axis=1)
    extra = jnp.concatenate([corner[0], corner[1]], axis=1)
    right = jnp.concatenate([quarter[2].reshape(96, TILE), quarter[3].reshape(96, TILE)], axis=1)
    one = dot3(jnp.concatenate([left, extra], axis=0), diag_ref[0])
    two = dot3(right, diag_ref[1])
    all_ref[pl.ds(r, 1)] = jnp.concatenate([one, two], axis=0).reshape(1, SHARD, 256)

    def shard_row(da, db):
        sx = (x + (1 - k) * da + k * db + 8) % 4
        sz = (z + k * da + (1 - k) * db + 8) % 4
        return sx * 8 + sz * 2 + k

    def part(da, db, h):
        return all_ref.at[shard_row(da, db), pl.ds(*HALF[h]), :]

    def pass_on(ref, sem, dev):
        remote(ref, ref, g_send, sem, dev).start()

    twin = (r + 1 - 2 * k, c)
    away = (0, -1, 1, 2)

    def to_line(d, h):
        pass_on(part(0, 0, h), first_recv.at[(0 if d == 1 else 2) + h], (shard_row(d, 0), c))

    def to_second(i, h):
        for d in (1, -1) if h == 0 else (-1, 1):
            sem = second_recv.at[i * 6 + (0 if d == 1 else 2) + h]
            pass_on(part(away[i], 0, h), sem, (shard_row(0, d), c))

    def came_first(kind, h):
        i = (1, 2, 3)[kind]
        ref = part(away[i], 0, h)
        wait_bytes(ref, first_recv.at[2 * kind + h])
        if (kind, h) == (0, 0):
            pass_on(ref, first_recv.at[4], (shard_row(1, 0), c))
        if (kind, h) == (1, 1):
            pass_on(ref, first_recv.at[5], (shard_row(-1, 0), c))
        to_second(i, h)
        pass_on(ref, twin_recv, twin)

    def came_second(i, kind, h):
        ref = part(away[i], (-1, 1, 2)[kind], h)
        wait_bytes(ref, second_recv.at[i * 6 + 2 * kind + h])
        if (kind, h) == (0, 0):
            pass_on(ref, second_recv.at[i * 6 + 4], (shard_row(0, 1), c))
        if (kind, h) == (1, 1):
            pass_on(ref, second_recv.at[i * 6 + 5], (shard_row(0, -1), c))
        pass_on(ref, twin_recv, twin)

    for h, d in ((0, 1), (1, -1), (1, 1), (0, -1)):
        to_line(d, h)
    for h in (0, 1):
        to_second(0, h)
    for h in (0, 1):
        pass_on(part(0, 0, h), twin_recv, twin)
    came_first(0, 0)
    came_first(1, 1)
    came_second(0, 0, 0)
    came_second(0, 1, 1)
    came_first(0, 1)
    came_first(1, 0)
    came_second(0, 0, 1)
    came_second(0, 1, 0)
    came_first(2, 0)
    came_first(2, 1)
    came_second(0, 2, 0)
    came_second(0, 2, 1)
    for i in (1, 2, 3):
        came_second(i, 0, 0)
        came_second(i, 1, 1)
        came_second(i, 0, 1)
        came_second(i, 1, 0)

    own.wait()
    wait_bytes(own_ref.at[pl.ds(0, 3)], o_recv)
    left = jnp.concatenate([own_ref[0].reshape(384, TILE), own_ref[1].reshape(384, TILE)], axis=1)
    right = jnp.concatenate([own_ref[2].reshape(384, TILE), own_ref[3].reshape(384, TILE)], axis=1)
    rows_ref[0] = dot3(left, diag_ref[0])
    rows_ref[1] = dot3(right, diag_ref[1])
    for i in (1, 2, 3):
        came_second(i, 2, 0)
        came_second(i, 2, 1)
    wait_bytes(all_ref.at[pl.ds(0, 16)], twin_recv)
    wait_bytes(all_ref.at[pl.ds(0, 31)], g_send)
    wait_bytes(own_ref.at[pl.ds(0, 3)], o_send)

    row_quarter = tiles.at[:, pl.ds(0, 32), :]
    holds_one = (r % 4) == c
    for j in range(4):

        @pl.when(jnp.logical_not(holds_one & ((r % 4) == j)))
        def _():
            wait_bytes(row_quarter, q_send)

    @pl.when(sends_corner)
    def _():
        @pl.loop(0, 63)
        def _(n):
            wait_bytes(corner.at[0], c_send)

        @pl.when(r == 3)
        def _():
            wait_bytes(corner.at[0], c_send)


def assemble(count, dest, slot, child, front, diag):
    any_space = pl.BlockSpec(memory_space=pl.ANY)
    vmem = pl.BlockSpec(memory_space=pltpu.VMEM)
    dma = pltpu.SemaphoreType.DMA
    return pl.pallas_call(
        assemble_kernel,
        out_shape=(
            pltpu.VMEM((72, TILE, TILE), F32),
            pltpu.VMEM((32, SHARD, 256), F32),
            pltpu.VMEM((2, 384, 256), F32),
            pltpu.VMEM((2, 256, 256), F32),
        ),
        in_specs=[pl.BlockSpec(memory_space=pltpu.SMEM)] + [any_space] * 5,
        out_specs=(vmem,) * 4,
        scratch_shapes=[
            pltpu.VMEM((1, 64), jnp.int32),
            pltpu.VMEM((1, 64), jnp.int32),
            pltpu.VMEM((64, TILE, TILE), F32),
            pltpu.VMEM((128, TILE, TILE), F32),
            pltpu.VMEM((EARLY, TILE, TILE), F32),
            pltpu.VMEM((128 - EARLY, TILE, TILE), F32),
            pltpu.VMEM((4, 3, TILE, TILE), F32),
            pltpu.VMEM((128, 1, 128), jnp.int32),
            pltpu.VMEM((128, 1, 128), jnp.int32),
            pltpu.VMEM((8, 128), jnp.int32),
            pltpu.VMEM((8, 128), jnp.int32),
            pltpu.SMEM((8, 128), jnp.int32),
            pltpu.SMEM((8, 128), jnp.int32),
            pltpu.VMEM((3, TILE, TILE), F32),
            pltpu.VMEM((4, 3, 32, TILE), F32),
            pltpu.VMEM((2, 8, TILE), F32),
            pltpu.SemaphoreType.REGULAR,
            pltpu.SemaphoreType.REGULAR,
            dma((2,)),
        ]
        + [dma] * 17
        + [dma((6,)), dma((24,)), dma, dma],
        compiler_params=pltpu.CompilerParams(
            collective_id=0, has_side_effects=True, vmem_limit_bytes=VMEM_LIMIT
        ),
        name="assemble",
    )(count, *[pltpu.with_memory_space_constraint(v, pltpu.HBM) for v in (dest, slot, child, front, diag)])


def update_kernel(field, all_ref, rows_ref, diag_ref, out_hbm, stage, row_parts, panel_ref, out_sem):
    r = lax.axis_index("row")
    c = lax.axis_index("col")
    corner = all_ref[:, 96:104, :].reshape(256, 256)
    both = halves(dot3(corner, diag_ref[1], ((0,), (0,))))
    p_one = rows_ref[0]
    p_two = rows_ref[1] - dot3(p_one, both)
    tile_row = (lax.broadcasted_iota(jnp.int32, (384, 1), 0) // TILE) * 32 + r
    zero = jnp.zeros_like(p_one)
    p_two = jnp.where(tile_row >= 2, p_two, zero)
    panel = jnp.where(
        c < 2,
        jnp.where(c == 0, p_one[:, :TILE], p_one[:, TILE:]),
        jnp.where(c == 2, p_two[:, :TILE], p_two[:, TILE:]),
    )
    panel_ref[...] = panel.reshape(3, TILE, TILE)
    second = jnp.where(tile_row >= 4, p_two, zero)
    first = jnp.where(tile_row >= 2, p_one, zero) - dot3(second, both, ((1,), (1,)))
    high, low = halves(jnp.concatenate([first, second], axis=1))
    row_parts[...] = jnp.concatenate([high, high, low], axis=1)

    @pl.loop(0, 4)
    def _(pair):
        shards = [pl.ds(pl.multiple_of(8 * pair + 4 * n, 4), 4) for n in range(2)]
        both_ways = [
            jnp.concatenate(
                [all_ref[rows, 32 * b + start : 32 * b + start + 32, :].reshape(TILE, 256) for rows in shards for b in range(3)]
            )
            for start in (0, 104)
        ]
        high, low = halves(jnp.concatenate(both_ways, axis=1))
        product = lax.dot_general(
            row_parts[...],
            jnp.concatenate([high, low, high], axis=1),
            (((1,), (1,)), ((), ())),
            preferred_element_type=F32,
        )
        for a in range(3):
            for n in range(2):
                for b in range(3):
                    across = TILE * (3 * n + b)
                    part = product[TILE * a : TILE * a + TILE, across : across + TILE]
                    stage[3 * a + b, 2 * pair + n] = field[3 * a + b, 2 * pair + n] - part

        @pl.when(pair == 0)
        def _():
            for a in range(3):
                stage[3 * a, 0] = panel_ref[a]

        done = pl.ds(2 * pair, 2)
        pltpu.make_async_copy(stage.at[:, done], out_hbm.at[:, done], out_sem).start()

    wait_bytes(stage, out_sem)


def update(field, gathered, rows, diag):
    vmem = pl.BlockSpec(memory_space=pltpu.VMEM)
    shape = (9, 8, TILE, TILE)
    return pl.pallas_call(
        update_kernel,
        out_shape=jax.ShapeDtypeStruct(shape, F32),
        in_specs=[vmem] * 4,
        out_specs=pl.BlockSpec(memory_space=pl.ANY),
        scratch_shapes=[
            pltpu.VMEM(shape, F32),
            pltpu.VMEM((384, 1536), BF16),
            pltpu.VMEM((3, TILE, TILE), F32),
            pltpu.SemaphoreType.DMA,
        ],
        compiler_params=pltpu.CompilerParams(vmem_limit_bytes=VMEM_LIMIT),
        name="update",
    )(field.reshape(shape), gathered, rows, diag)


def body(front, child_tiles, tile_dest, tile_slot, tile_count, diag_inverses):
    field, gathered, rows, diag = assemble(
        tile_count,
        tile_dest.reshape(1, 64),
        tile_slot.reshape(1, 64),
        child_tiles,
        front.reshape(72, TILE, TILE),
        diag_inverses,
    )
    return update(field, gathered, rows, diag).reshape(front.shape)


def solution(mesh):
    return jax.shard_map(
        body,
        mesh=mesh,
        in_specs=(
            P(None, "row", None, "col", None, None),
            P(("row", "col"), None, None),
            P(("row", "col"), None),
            P(("row", "col")),
            P(("row", "col")),
            P(),
        ),
        out_specs=P(None, "row", None, "col", None, None),
        check_vma=False,
    )
```

time: 168 us -> 147 us (0.88); the launches traced: 165 us -> 147 us
  Pallas kernels: 163 us -> 146 us
    pallas_call x2, Pallas kernels: 163 us -> 146 us  [the longest x1 140 us: assemble(): pl.pallas_call(assemble_kernel, out_shape=(pltpu.VMEM((72, TILE, TILE), F...]
where the time goes in v3:
time: 147 us
  Pallas kernels  146 us (99%)
    pallas_call x1, Pallas kernels, assemble(): pl.pallas_call(assemble_kernel, out_shape=(pltpu.VMEM((72, TILE, TILE), F...  140 us
    pallas_call x1, Pallas kernels, update(): pl.pallas_call(update_kernel, out_shape=jax.ShapeDtypeStruct(shape, F32),...  6.59 us

profile of v3, /device:TPU:1, one launch (start us, length us, event | category | flops | bytes accessed | tf_op | source)
XLA Modules:
  0.0 147.0 jit_solution(12097022830789162688)
XLA Ops:
  0.7 139.8 %assemble.1 = (f32[72,128,128]{2,1,0:T(8,128)S(1)}, f32[32,200,256]{2,1,0:T(8,128)S(1)}, f32[2,384,256]{2,1,0:T(8,128)S(1)}, f32[2,256,256]{2,1,0:T(8,128)S(1)}) custom-call(s32[1]{0:T(128)S(6)} %copy.8.count_ref, s32[1,64]{1,0:T(1,128)} %bitcast.9, s32[1,64]{1,0:T(1,128)} %bitcast.10, f32[64,128,128]{2,1,0:T(8,128)} %child_hbm.1, f32[72,128,128]{2,1,0:T(8,128)} %bitcast.8, ...), custom_call_target="tpu_custom_call" | custom-call | tf_op jit(solution)/shard_map/assemble/pallas_call | solution.py:426
  140.4 6.6 %update.1 = f32[9,8,128,128]{3,2,1,0:T(8,128)} custom-call(f32[9,8,128,128]{3,2,1,0:T(8,128)S(1)} %bitcast.7, f32[32,200,256]{2,1,0:T(8,128)S(1)} %get-tuple-element.10.all_ref, f32[2,384,256]{2,1,0:T(8,128)S(1)} %get-tuple-element.11.rows_ref, f32[2,256,256]{2,1,0:T(8,128)S(1)} %get-tuple-element.12.diag_ref), custom_call_target="tpu_custom_call" | custom-call | tf_op jit(solution)/shard_map/update/pallas_call | solution.py:524

commit v4 on v3

--- a/solution.py
+++ b/solution.py
@@ -14,7 +14,7 @@
 TILE = 128
 FIRST = 12
 EARLY = 96
-HALF = ((0, 104), (104, 96))
+PIECES = ((0, 56), (56, 48), (104, 48), (152, 48))
 SHARD = 200
 
 
@@ -127,9 +127,11 @@
     slot_ref,
     child,
     packed,
+    summed,
     incoming,
     incoming_late,
     own_ref,
+    diag_parts,
     code_rows,
     code_in,
     rows,
@@ -239,19 +241,30 @@
     to_scalars.wait()
     front_load.wait()
     diag_load.wait()
-    wait_bytes(packed.at[pl.ds(0, last)], tile_send)
+    for n in range(2):
+        high, low = halves(diag_ref[n])
+        diag_parts[n] = jnp.concatenate([high, low, high], axis=0)
+
+    def by_diag(a, n):
+        high, low = halves(a)
+        return lax.dot_general(
+            jnp.concatenate([high, high, low], axis=1),
+            diag_parts[n],
+            (((1,), (0,)), ((), ())),
+            preferred_element_type=F32,
+        )
 
     def sums(buffer, start, count):
         def run(t, total):
             tile = buffer[order[0, t]]
             total = jnp.where(order[1, t] > 0, tile, total + tile)
-            packed[t] = total
+            summed[t] = total
             return total
 
         lax.fori_loop(start, start + count, run, jnp.zeros((TILE, TILE), F32))
 
     def assembled(q, n):
-        added = packed.at[pl.ds(EARLY * n, (EARLY, 128 - EARLY)[n])][order[2 + n, q]]
+        added = summed.at[pl.ds(EARLY * n, (EARLY, 128 - EARLY)[n])][order[2 + n, q]]
         return field[q] + jnp.where(order[4 + n, q] > 0, added, 0.0)
 
     wait_bytes(incoming, tile_recv)
@@ -317,8 +330,8 @@
     left = jnp.concatenate([quarter[0].reshape(96, TILE), quarter[1].reshape(96, TILE)], axis=1)
     extra = jnp.concatenate([corner[0], corner[1]], axis=1)
     right = jnp.concatenate([quarter[2].reshape(96, TILE), quarter[3].reshape(96, TILE)], axis=1)
-    one = dot3(jnp.concatenate([left, extra], axis=0), diag_ref[0])
-    two = dot3(right, diag_ref[1])
+    one = by_diag(jnp.concatenate([left, extra], axis=0), 0)
+    two = by_diag(right, 1)
     all_ref[pl.ds(r, 1)] = jnp.concatenate([one, two], axis=0).reshape(1, SHARD, 256)
 
     def shard_row(da, db):
@@ -326,80 +339,78 @@
         sz = (z + k * da + (1 - k) * db + 8) % 4
         return sx * 8 + sz * 2 + k
 
-    def part(da, db, h):
-        return all_ref.at[shard_row(da, db), pl.ds(*HALF[h]), :]
+    def piece(da, db, p):
+        return all_ref.at[shard_row(da, db), pl.ds(*PIECES[p]), :]
 
     def pass_on(ref, sem, dev):
         remote(ref, ref, g_send, sem, dev).start()
 
     twin = (r + 1 - 2 * k, c)
     away = (0, -1, 1, 2)
-
-    def to_line(d, h):
-        pass_on(part(0, 0, h), first_recv.at[(0 if d == 1 else 2) + h], (shard_row(d, 0), c))
-
-    def to_second(i, h):
-        for d in (1, -1) if h == 0 else (-1, 1):
-            sem = second_recv.at[i * 6 + (0 if d == 1 else 2) + h]
-            pass_on(part(away[i], 0, h), sem, (shard_row(0, d), c))
-
-    def came_first(kind, h):
-        i = (1, 2, 3)[kind]
-        ref = part(away[i], 0, h)
-        wait_bytes(ref, first_recv.at[2 * kind + h])
-        if (kind, h) == (0, 0):
-            pass_on(ref, first_recv.at[4], (shard_row(1, 0), c))
-        if (kind, h) == (1, 1):
-            pass_on(ref, first_recv.at[5], (shard_row(-1, 0), c))
-        to_second(i, h)
+    count = len(PIECES)
+    up = range(count // 2)
+    down = range(count // 2, count)
+
+    def to_second(i, p):
+        for d in (1, -1) if p in up else (-1, 1):
+            sem = second_recv.at[(3 * i + (0 if d == 1 else 1)) * count + p]
+            pass_on(piece(away[i], 0, p), sem, (shard_row(0, d), c))
+
+    def came_first(way, p):
+        ref = piece(away[way + 1], 0, p)
+        wait_bytes(ref, first_recv.at[way * count + p])
+        if way == 0 and p in up:
+            pass_on(ref, first_recv.at[2 * count + p], (shard_row(1, 0), c))
+        if way == 1 and p in down:
+            pass_on(ref, first_recv.at[2 * count + p], (shard_row(-1, 0), c))
+        to_second(way + 1, p)
         pass_on(ref, twin_recv, twin)
 
-    def came_second(i, kind, h):
-        ref = part(away[i], (-1, 1, 2)[kind], h)
-        wait_bytes(ref, second_recv.at[i * 6 + 2 * kind + h])
-        if (kind, h) == (0, 0):
-            pass_on(ref, second_recv.at[i * 6 + 4], (shard_row(0, 1), c))
-        if (kind, h) == (1, 1):
-            pass_on(ref, second_recv.at[i * 6 + 5], (shard_row(0, -1), c))
+    def came_second(i, way, p):
+        ref = piece(away[i], (-1, 1, 2)[way], p)
+        wait_bytes(ref, second_recv.at[(3 * i + way) * count + p])
+        if way == 0 and p in up:
+            pass_on(ref, second_recv.at[(3 * i + 2) * count + p], (shard_row(0, 1), c))
+        if way == 1 and p in down:
+            pass_on(ref, second_recv.at[(3 * i + 2) * count + p], (shard_row(0, -1), c))
         pass_on(ref, twin_recv, twin)
 
-    for h, d in ((0, 1), (1, -1), (1, 1), (0, -1)):
-        to_line(d, h)
-    for h in (0, 1):
-        to_second(0, h)
-    for h in (0, 1):
-        pass_on(part(0, 0, h), twin_recv, twin)
-    came_first(0, 0)
-    came_first(1, 1)
-    came_second(0, 0, 0)
-    came_second(0, 1, 1)
-    came_first(0, 1)
-    came_first(1, 0)
-    came_second(0, 0, 1)
-    came_second(0, 1, 0)
-    came_first(2, 0)
-    came_first(2, 1)
-    came_second(0, 2, 0)
-    came_second(0, 2, 1)
+    passed = [(way, pair[way]) for pair in zip(up, down) for way in (0, 1)]
+    kept = [(way, pair[1 - way]) for pair in zip(up, down) for way in (0, 1)]
+    for way, p in passed + kept:
+        d = 1 - 2 * way
+        pass_on(piece(0, 0, p), first_recv.at[way * count + p], (shard_row(d, 0), c))
+    for p in range(count):
+        to_second(0, p)
+    for p in range(count):
+        pass_on(piece(0, 0, p), twin_recv, twin)
+    for some in (passed, kept):
+        for way, p in some:
+            came_first(way, p)
+        for way, p in some:
+            came_second(0, way, p)
+    for p in range(count):
+        came_first(2, p)
+    for p in range(count):
+        came_second(0, 2, p)
     for i in (1, 2, 3):
-        came_second(i, 0, 0)
-        came_second(i, 1, 1)
-        came_second(i, 0, 1)
-        came_second(i, 1, 0)
-
+        for way, p in passed + kept:
+            came_second(i, way, p)
+
+    for i in (1, 2, 3):
+        for p in range(count):
+            came_second(i, 2, p)
     own.wait()
     wait_bytes(own_ref.at[pl.ds(0, 3)], o_recv)
     left = jnp.concatenate([own_ref[0].reshape(384, TILE), own_ref[1].reshape(384, TILE)], axis=1)
     right = jnp.concatenate([own_ref[2].reshape(384, TILE), own_ref[3].reshape(384, TILE)], axis=1)
-    rows_ref[0] = dot3(left, diag_ref[0])
-    rows_ref[1] = dot3(right, diag_ref[1])
-    for i in (1, 2, 3):
-        came_second(i, 2, 0)
-        came_second(i, 2, 1)
+    rows_ref[0] = by_diag(left, 0)
+    rows_ref[1] = by_diag(right, 1)
     wait_bytes(all_ref.at[pl.ds(0, 16)], twin_recv)
     wait_bytes(all_ref.at[pl.ds(0, 31)], g_send)
     wait_bytes(own_ref.at[pl.ds(0, 3)], o_send)
 
+    wait_bytes(packed.at[pl.ds(0, last)], tile_send)
     row_quarter = tiles.at[:, pl.ds(0, 32), :]
     holds_one = (r % 4) == c
     for j in range(4):
@@ -438,9 +449,11 @@
             pltpu.VMEM((1, 64), jnp.int32),
             pltpu.VMEM((64, TILE, TILE), F32),
             pltpu.VMEM((128, TILE, TILE), F32),
+            pltpu.VMEM((128, TILE, TILE), F32),
             pltpu.VMEM((EARLY, TILE, TILE), F32),
             pltpu.VMEM((128 - EARLY, TILE, TILE), F32),
             pltpu.VMEM((4, 3, TILE, TILE), F32),
+            pltpu.VMEM((2, 768, 256), BF16),
             pltpu.VMEM((128, 1, 128), jnp.int32),
             pltpu.VMEM((128, 1, 128), jnp.int32),
             pltpu.VMEM((8, 128), jnp.int32),
@@ -455,7 +468,7 @@
             dma((2,)),
         ]
         + [dma] * 17
-        + [dma((6,)), dma((24,)), dma, dma],
+        + [dma((12,)), dma((48,)), dma, dma],
         compiler_params=pltpu.CompilerParams(
             collective_id=0, has_side_effects=True, vmem_limit_bytes=VMEM_LIMIT
         ),

time: 147 us -> 146 us (level)
  no operation moved by 1% of the time
where the time goes in v4:
time: 146 us
  Pallas kernels  145 us (99%)
    pallas_call x1, Pallas kernels, assemble(): pl.pallas_call(assemble_kernel, out_shape=(pltpu.VMEM((72, TILE, TILE), F...  139 us
    pallas_call x1, Pallas kernels, update(): pl.pallas_call(update_kernel, out_shape=jax.ShapeDtypeStruct(shape, F32),...  6.59 us

profile of v4, /device:TPU:1, one launch (start us, length us, event | category | flops | bytes accessed | tf_op | source)
XLA Modules:
  0.0 146.1 jit_solution(4025580010791293430)
XLA Ops:
  0.7 138.8 %assemble.1 = (f32[72,128,128]{2,1,0:T(8,128)S(1)}, f32[32,200,256]{2,1,0:T(8,128)S(1)}, f32[2,384,256]{2,1,0:T(8,128)S(1)}, f32[2,256,256]{2,1,0:T(8,128)S(1)}) custom-call(s32[1]{0:T(128)S(6)} %copy.8.count_ref, s32[1,64]{1,0:T(1,128)} %bitcast.9, s32[1,64]{1,0:T(1,128)} %bitcast.10, f32[64,128,128]{2,1,0:T(8,128)} %child_hbm.1, f32[72,128,128]{2,1,0:T(8,128)} %bitcast.8, ...), custom_call_target="tpu_custom_call" | custom-call | tf_op jit(solution)/shard_map/assemble/pallas_call | solution.py:437
  139.5 6.6 %update.1 = f32[9,8,128,128]{3,2,1,0:T(8,128)} custom-call(f32[9,8,128,128]{3,2,1,0:T(8,128)S(1)} %bitcast.7, f32[32,200,256]{2,1,0:T(8,128)S(1)} %get-tuple-element.10.all_ref, f32[2,384,256]{2,1,0:T(8,128)S(1)} %get-tuple-element.11.rows_ref, f32[2,256,256]{2,1,0:T(8,128)S(1)} %get-tuple-element.12.diag_ref), custom_call_target="tpu_custom_call" | custom-call | tf_op jit(solution)/shard_map/update/pallas_call | solution.py:537

commit v5 on v4

--- a/solution.py
+++ b/solution.py
@@ -297,21 +297,23 @@
 
     @pl.when(sends_corner)
     def _():
-        @pl.loop(0, 64)
-        def _(n):
-            i = n // 4
-            tr = i + 16 * (r - 2)
-            tc = n % 4
-            src = tiles.at[0, pl.ds(pl.multiple_of(i * 8, 8), 8), :]
-            mine = (tr == r) & (tc == c)
-
-            @pl.when(mine)
-            def _():
-                pltpu.make_async_copy(src, corner.at[c], c_recv).start()
-
-            @pl.when(jnp.logical_not(mine))
-            def _():
-                remote(src, corner.at[c], c_send, c_recv, (tr, tc)).start()
+        for i in range(16):
+            src = tiles.at[0, 8 * i : 8 * i + 8, :]
+            for tc in range(4):
+                dev = (i + 16 * (r - 2), tc)
+                copy = remote(src, corner.at[c], c_send, c_recv, dev)
+                if i != 2:
+                    copy.start()
+                    continue
+                mine = (r == 2) & (c == tc)
+
+                @pl.when(mine)
+                def _():
+                    pltpu.make_async_copy(src, corner.at[c], c_recv).start()
+
+                @pl.when(jnp.logical_not(mine))
+                def _():
+                    copy.start()
 
     for a in range(3):
 

time: 146 us -> 146 us (level)
  no operation moved by 1% of the time
where the time goes in v5:
time: 146 us
  Pallas kernels  145 us (99%)
    pallas_call x1, Pallas kernels, assemble(): pl.pallas_call(assemble_kernel, out_shape=(pltpu.VMEM((72, TILE, TILE), F...  138 us
    pallas_call x1, Pallas kernels, update(): pl.pallas_call(update_kernel, out_shape=jax.ShapeDtypeStruct(shape, F32),...  6.59 us

profile of v5, /device:TPU:1, one launch (start us, length us, event | category | flops | bytes accessed | tf_op | source)
XLA Modules:
  0.0 145.7 jit_solution(14524006119616392829)
XLA Ops:
  0.7 138.5 %assemble.1 = (f32[72,128,128]{2,1,0:T(8,128)S(1)}, f32[32,200,256]{2,1,0:T(8,128)S(1)}, f32[2,384,256]{2,1,0:T(8,128)S(1)}, f32[2,256,256]{2,1,0:T(8,128)S(1)}) custom-call(s32[1]{0:T(128)S(6)} %copy.8.count_ref, s32[1,64]{1,0:T(1,128)} %bitcast.9, s32[1,64]{1,0:T(1,128)} %bitcast.10, f32[64,128,128]{2,1,0:T(8,128)} %child_hbm.1, f32[72,128,128]{2,1,0:T(8,128)} %bitcast.8, ...), custom_call_target="tpu_custom_call" | custom-call | tf_op jit(solution)/shard_map/assemble/pallas_call | solution.py:439
  139.1 6.6 %update.1 = f32[9,8,128,128]{3,2,1,0:T(8,128)} custom-call(f32[9,8,128,128]{3,2,1,0:T(8,128)S(1)} %bitcast.7, f32[32,200,256]{2,1,0:T(8,128)S(1)} %get-tuple-element.10.all_ref, f32[2,384,256]{2,1,0:T(8,128)S(1)} %get-tuple-element.11.rows_ref, f32[2,256,256]{2,1,0:T(8,128)S(1)} %get-tuple-element.12.diag_ref), custom_call_target="tpu_custom_call" | custom-call | tf_op jit(solution)/shard_map/update/pallas_call | solution.py:539

commit v6 on v5

--- a/solution.py
+++ b/solution.py
@@ -98,12 +98,13 @@
     ah, al = a if isinstance(a, tuple) else halves(a)
     bh, bl = b if isinstance(b, tuple) else halves(b)
 
-    def dot(u, v):
-        return lax.dot_general(u, v, (dims, ((), ())), preferred_element_type=F32)
-
-    if dims == ((1,), (0,)):
-        return dot(jnp.concatenate([ah, ah, al], axis=1), jnp.concatenate([bh, bl, bh], axis=0))
-    return dot(ah, bh) + (dot(ah, bl) + dot(al, bh))
+    (da,), (db,) = dims
+    return lax.dot_general(
+        jnp.concatenate([ah, ah, al], axis=da),
+        jnp.concatenate([bh, bl, bh], axis=db),
+        (dims, ((), ())),
+        preferred_element_type=F32,
+    )
 
 
 def to_rows(column):

time: 146 us -> 146 us (level)
  no operation moved by 1% of the time
where the time goes in v6:
time: 146 us
  Pallas kernels  145 us (99%)
    pallas_call x1, Pallas kernels, assemble(): pl.pallas_call(assemble_kernel, out_shape=(pltpu.VMEM((72, TILE, TILE), F...  138 us
    pallas_call x1, Pallas kernels, update(): pl.pallas_call(update_kernel, out_shape=jax.ShapeDtypeStruct(shape, F32),...  6.57 us

profile of v6, /device:TPU:1, one launch (start us, length us, event | category | flops | bytes accessed | tf_op | source)
XLA Modules:
  0.0 145.7 jit_solution(3076867700014368779)
XLA Ops:
  0.7 138.5 %assemble.1 = (f32[72,128,128]{2,1,0:T(8,128)S(1)}, f32[32,200,256]{2,1,0:T(8,128)S(1)}, f32[2,384,256]{2,1,0:T(8,128)S(1)}, f32[2,256,256]{2,1,0:T(8,128)S(1)}) custom-call(s32[1]{0:T(128)S(6)} %copy.8.count_ref, s32[1,64]{1,0:T(1,128)} %bitcast.9, s32[1,64]{1,0:T(1,128)} %bitcast.10, f32[64,128,128]{2,1,0:T(8,128)} %child_hbm.1, f32[72,128,128]{2,1,0:T(8,128)} %bitcast.8, ...), custom_call_target="tpu_custom_call" | custom-call | tf_op jit(solution)/shard_map/assemble/pallas_call | solution.py:440
  139.1 6.6 %update.1 = f32[9,8,128,128]{3,2,1,0:T(8,128)} custom-call(f32[9,8,128,128]{3,2,1,0:T(8,128)S(1)} %bitcast.7, f32[32,200,256]{2,1,0:T(8,128)S(1)} %get-tuple-element.10.all_ref, f32[2,384,256]{2,1,0:T(8,128)S(1)} %get-tuple-element.11.rows_ref, f32[2,256,256]{2,1,0:T(8,128)S(1)} %get-tuple-element.12.diag_ref), custom_call_target="tpu_custom_call" | custom-call | tf_op jit(solution)/shard_map/update/pallas_call | solution.py:540
